TPU v7x, 768 devices: a whole 4x8x12 slice. The times are simulated.
768 devices in a mesh: fsdp: 32 (over z_hi, x, core), dp: 24 (over y, z_lo).
Axes of the slice: x: 4, y: 8, z: 12 (z_hi: 4, z_lo: 3; z = z_hi * 3 + z_lo), core: 2. Of those that a mesh axis runs over, the one named last changes fastest.
Arguments:
- hidden: bfloat16 [24, 8192, 5120], P('dp', 'fsdp'), may hold values from -6 to 6
- queries: bfloat16 [24, 8192, 2560], P('dp', 'fsdp'), may hold values from -100 to 100
- keys: bfloat16 [24, 8192, 512], P('dp', 'fsdp'), may hold values from -4 to 4
- value_weight: bfloat16 [5120, 512], P('fsdp'), may hold values from -0.078125 to 0.078125
- value_head: bfloat16 [2560], replicated, may hold values from -0.8984375 to 0.8984375
- lengths: int32 [24, 32, 4], P('dp', 'fsdp'), may hold values from 1 to 128, 256 in all within a row
- plan: int32 [24, 128], P('dp', 'fsdp'), may hold values from 0 to 127, each once within a row
- targets: float32 [24, 8192], P('dp', 'fsdp'), may hold values from -5 to 5
- loss_mask: int32 [24, 8192], P('dp', 'fsdp'), may hold values 0 or 1
Outputs:
- values: float32 [24, 8192], P('dp', 'fsdp')
- seq_values: float32 [24, 128], P('dp', 'fsdp')
- d_weight: bfloat16 [5120, 512], P('fsdp')
Inputs may be any that keep to these rules, and one draw needn't show every extreme that they name: The 4 lengths of a device sum to 256. `plan`: each data group's row names every slot once.
All inputs are finite; a program needn't handle non-finite values. No bound on the sum of `loss_mask` on one device may be relied on, other than what follows from the above.
Results may differ from a plain program's by a relative error of at most 0.02.
Values may be sent and summed in bfloat16 or wider, within the bound.
No kernel may reach another device: no remote copies, remote signals or barrier semaphores. Data moves between devices by JAX's collectives and lax.ppermute only.
A program may use at most 64 MiB of HBM per device.

v0:
```python
import math

import jax
import jax.numpy as jnp
from jax import lax
from jax.sharding import PartitionSpec as P

KVH = 4
QPK = 5
HD = 128
SEQ_DEV = 4


def segment_ids(lengths, rows):
    ends = jnp.cumsum(lengths)
    position = jnp.arange(rows, dtype=jnp.int32)
    return jnp.sum((position[:, None] >= ends[None, :]).astype(jnp.int32), axis=1)


def local(hidden, queries, keys, value_weight, value_head, lengths, plan, targets, loss_mask):
    x_rows = hidden[0]
    rows = x_rows.shape[0]
    width = value_weight.shape[1]
    total_tokens = rows * lax.axis_size("fsdp") * lax.axis_size("dp")
    grad_scale = 1.0 / math.sqrt(total_tokens)
    full_weight = lax.all_gather(value_weight, "fsdp", axis=0, tiled=True)
    projected = jnp.dot(x_rows, full_weight, preferred_element_type=jnp.float32)
    proj = projected.astype(jnp.bfloat16)
    own_lengths = lengths[0, 0]
    seg = segment_ids(own_lengths, rows)
    q4 = queries[0].reshape(rows, KVH, QPK, HD)
    k3 = keys[0].reshape(rows, KVH, HD)
    v3 = proj.reshape(rows, KVH, HD)
    head3 = value_head.reshape(KVH, QPK, HD).astype(jnp.float32)
    score = jnp.einsum("tgph,sgh->gpts", q4, k3, preferred_element_type=jnp.float32) * (
        1.0 / math.sqrt(HD)
    )
    position = jnp.arange(rows, dtype=jnp.int32)
    allowed = (seg[:, None] == seg[None, :]) & (position[None, :] <= position[:, None])
    score = jnp.where(allowed[None, None], score, -jnp.inf)
    top = jnp.max(score, axis=-1, keepdims=True)
    expo = jnp.exp(score - top)
    probs = (expo / jnp.sum(expo, axis=-1, keepdims=True)).astype(jnp.bfloat16)
    mixed = jnp.einsum("gpts,sgh->tgph", probs, v3, preferred_element_type=jnp.float32)
    token_values = jnp.einsum("tgph,gph->t", mixed, head3)
    slot_hits = (seg[:, None] == jnp.arange(SEQ_DEV, dtype=jnp.int32)[None, :]).astype(jnp.float32)
    slot_mean = jnp.sum(slot_hits * token_values[:, None], axis=0) / own_lengths.astype(jnp.float32)
    every_mean = lax.all_gather(slot_mean, "fsdp", axis=0, tiled=True)
    picker = (plan[0][:, None] == jnp.arange(every_mean.shape[0], dtype=jnp.int32)[None, :]).astype(
        jnp.float32
    )
    seq_values = jnp.sum(picker * every_mean[None, :], axis=1)
    resid = jnp.where(loss_mask[0] == 1, token_values - targets[0], 0.0) * grad_scale
    d_mixed = (resid[:, None, None, None] * head3[None]).astype(jnp.bfloat16)
    d_proj = jnp.einsum("gpts,tgph->sgh", probs, d_mixed, preferred_element_type=jnp.float32)
    d_proj = d_proj.astype(jnp.bfloat16).reshape(rows, width)
    group_sum = lax.psum_scatter(
        jnp.dot(x_rows.T, d_proj, preferred_element_type=jnp.float32).astype(jnp.bfloat16),
        "fsdp",
        scatter_dimension=0,
        tiled=True,
    )
    group_grad = lax.optimization_barrier(group_sum).astype(jnp.float32)
    d_weight = lax.psum(group_grad.astype(jnp.bfloat16), "dp")
    return (token_values[None, :], seq_values[None, :], d_weight)


def solution(mesh):
    in_specs = (
        P("dp", "fsdp", None),
        P("dp", "fsdp", None),
        P("dp", "fsdp", None),
        P("fsdp", None),
        P(),
        P("dp", "fsdp", None),
        P("dp", "fsdp"),
        P("dp", "fsdp"),
        P("dp", "fsdp"),
    )
    out_specs = (P("dp", "fsdp"), P("dp", "fsdp"), P("fsdp", None))
    return jax.shard_map(local, mesh=mesh, in_specs=in_specs, out_specs=out_specs, check_vma=False)
```

profile of v0, /device:TPU:204, one launch (start us, length us, event | category | flops | bytes accessed | tf_op | source)
XLA Modules:
  0.0 511.4 jit_solution(1547010692819933564)
XLA Ops:
  7.2 0.7 all-gather.2.cloned.1.call-update
  8.0 0.7 reshape.97
  8.7 0.7 reshape.110
  9.4 1.0 reshape_squeeze.6
  10.4 2.4 copy.28
  12.8 0.2 reduce-window.8
  13.2 5.3 %fusion.34 = (f32[4,5,256]{2,1,0:T(8,128)S(1)}, f32[4,5,256,256]{2,3,1,0:T(8,128)}) fusion(pred[256,256]{0,1:T(8,128)(4,1)S(1)} %fusion.23, bf16[256,4,5,128]{0,3,2,1:T(8,128)(2,1)} %bitcast.62, bf16[256,4,128,1]{2,1,0,3:T(4,128)(2,1)S(1)} %bitcast.65), kind=kOutput, calls=%fused_computation.41 | convolution fusion | flops 340787456 | bytes 6901760 | tf_op jit(solution)/shard_map/sub | solution.py:42
  18.6 4.6 divide_convert_fusion
  23.2 82.2 %all-gather.2.cloned.1.call-done = bf16[5120,512]{1,0:T(8,128)(2,1)} async-done(((bf16[160,512]{1,0:T(8,128)(2,1)}), bf16[5120,512]{1,0:T(8,128)(2,1)}) %all-gather.2.cloned.1.call-update) | async-done | bytes 5242896 | tf_op jit(solution)/shard_map/all_gather | solution.py:26
  105.4 4.0 fusion.18
  109.4 0.1 copy.43
  109.6 2.5 fusion.3
  112.1 2.7 fusion.17
  114.9 3.9 fusion.1
  118.8 7.9 %copy.46 = bf16[5120,512]{1,0:T(8,128)(2,1)} copy(bf16[5120,512]{0,1:T(8,128)(2,1)} %fusion.1) | data formatting | bytes 10485760
  126.8 1.3 dynamic-slice
  128.7 0.1 select_reduce_fusion
  128.8 130.9 %reduce-scatter.4.cloned.1.call-done = bf16[160,512]{1,0:T(8,128)(2,1)} async-done(((bf16[5120,512]{1,0:T(8,128)(2,1)}), bf16[160,512]{1,0:T(8,128)(2,1)}) %reduce-scatter.4.cloned.1.call-update) | async-done | bytes 163856
  259.8 1.7 copy.47
  261.6 0.1 fusion.31
  261.7 66.0 %all-reduce = f32[128]{0:T(128)S(1)} all-reduce(f32[128]{0:T(128)S(1)} %fusion.31), channel_id=1, replica_groups=mesh['fsdp'=32,'dp'=24] {'fsdp'}, use_global_device_ids=true, to_apply=%add | all-reduce | flops 128 | bytes 1024
  327.7 0.7 select_reduce_fusion.1
  328.4 174.8 %all-reduce.3.cloned.1.call-done = bf16[160,512]{0,1:T(8,128)(2,1)} async-done(((bf16[160,512]{0,1:T(8,128)(2,1)}), bf16[160,512]{0,1:T(8,128)(2,1)}) %all-reduce.3.cloned.1.call-update) | async-done | bytes 163856 | tf_op jit(solution)/shard_map/psum | solution.py:64
  503.2 1.7 copy.34
  (23 shorter events, 0.4 us)
Async XLA Ops:
  7.2 98.3 %copy-start = (bf16[1,256,5120]{2,1,0:T(8,128)(2,1)S(1)}, bf16[1,256,5120]{2,1,0:T(8,128)(2,1)}, u32[]{:S(2)}) copy-start(bf16[1,256,5120]{2,1,0:T(8,128)(2,1)} %param.9) | copy-start | bytes 7864324
  7.2 5.7 %copy-start.3 = (s32[1,1,4]{2,1,0:T(1,128)S(1)}, s32[1,1,4]{2,1,0:T(1,128)}, u32[]{:S(2)}) copy-start(s32[1,1,4]{2,1,0:T(1,128)} %param.14) | copy-start | bytes 52
  7.2 5.8 %copy-start.4 = (s32[1,256]{1,0:T(1,128)S(1)}, s32[1,256]{1,0:T(1,128)}, u32[]{:S(2)}) copy-start(s32[1,256]{1,0:T(1,128)} %param.17) | copy-start | bytes 3076
  7.2 98.2 %all-gather.2.cloned.1.call-start = ((), (), s32[]{:S(2)}) async-start(), calls=%async_computation.1 | async-start | bytes 5406720 | tf_op jit(solution)/shard_map/all_gather | solution.py:26
  7.9 251.9 %reduce-scatter.4.cloned.1.call-start = ((), (), s32[]{:S(2)}) async-start(), calls=%async_computation.3 | async-start | bytes 5406720
  109.4 2.7 copy-start.2
  112.1 16.6 %copy-start.1 = (f32[1,256,1,1]{1,0,3,2:T(1,128)}, f32[1,256,1,1]{1,0,3,2:T(1,128)S(1)}, u32[]{:S(2)}) copy-start(f32[1,256,1,1]{1,0,3,2:T(1,128)S(1)} %fusion.3) | copy-start | bytes 3076
  126.7 201.0 %copy-start.5 = (s32[1,4]{1,0:T(1,128)S(1)}, s32[1,4]{1,0:T(1,128)}, u32[]{:S(2)}) copy-start(s32[1,4]{1,0:T(1,128)} %param.15) | copy-start | bytes 52
  126.7 376.4 %all-reduce.3.cloned.1.call-start = ((), (), s32[]{:S(2)}) async-start(), calls=%async_computation.2 | async-start | bytes 524288 | tf_op jit(solution)/shard_map/psum | solution.py:64
Sparse Core Ops, SparseCore 0:
  11.7 93.6 all-gather.1
  126.9 132.8 reduce-scatter.3
  263.0 240.1 all-reduce.2
where the time goes:
time: 512 us; the launch traced here: 511 us
  waiting for transfers between devices  389 us (76%)
  blocking collectives  66 us (13%)
  matrix products  18.5 us (4%)
  local copies, waits for them, and re-layouts  17.7 us (3%)
  between operations  14.5 us (3%)
  other arithmetic  5.92 us (1%)
    psum x1, waiting for transfers between devices, local(): d_weight = lax.psum(group_grad.astype(jnp.bfloat16), 'dp')  175 us
    unnamed x4, waiting for transfers between devices  132 us
    all_gather x1, waiting for transfers between devices, local(): full_weight = lax.all_gather(value_weight, 'fsdp', axis=0, tiled=True)  82.2 us
    unnamed x1, blocking collectives  66 us
    unnamed x18, local copies, waits for them, and re-layouts  15.2 us
  transfers between devices with their start and end apart: 3, of which 3 were waited for; matrix products, arithmetic and copies ran while one was open for 3% of the time, Pallas kernels for 0%

commit v1 on v0

v1 whole, which is shorter than its diff:
```python
import functools
import math

import jax
import jax.numpy as jnp
from jax import lax
from jax.experimental import pallas as pl
from jax.experimental.pallas import tpu as pltpu
from jax.sharding import PartitionSpec as P

KVH = 4
QPK = 5
QH = KVH * QPK
HD = 128
SEQ_DEV = 4
GR = 8
HROWS = KVH * GR
PIECE = 160
PROWS = HROWS + 8
TAIL = 32

NT = (((1,), (1,)), ((), ()))
NN = (((1,), (0,)), ((), ()))
TN = (((0,), (0,)), ((), ()))
VMEM = pltpu.CompilerParams(vmem_limit_bytes=24 * 1024 * 1024)


def dot(a, b, dims):
    return lax.dot_general(a, b, dims, preferred_element_type=jnp.float32)


def split(x):
    high = x.astype(jnp.bfloat16)
    return high, (x - high.astype(jnp.float32)).astype(jnp.bfloat16)


def lane_group(rows):
    return lax.broadcasted_iota(jnp.int32, (rows, HD), 1) // TAIL


def turn(x, shift):
    shift = shift % HD
    return x if shift == 0 else pltpu.roll(x, shift, 1)


def head_rows(head_ref, g):
    row = lax.broadcasted_iota(jnp.int32, (GR, HD), 0)
    out = jnp.zeros((GR, HD), jnp.float32)
    for p in range(QPK):
        q = g * QPK + p
        line = head_ref[0:1, q * HD : (q + 1) * HD].astype(jnp.float32)
        out = jnp.where(row == p, jnp.broadcast_to(line, (GR, HD)), out)
    return out


def pack_tail(parts, r):
    group = lane_group(GR)
    tail = jnp.zeros((GR, HD), jnp.float32)
    for g in range(KVH):
        tail = jnp.where(group == g, turn(parts[g], TAIL * (g - r)), tail)
    return tail


def fold_kernel(w_ref, head_ref, out_ref):
    n = out_ref.shape[0]
    mains, tails = [], []
    for g in range(KVH):
        head = head_rows(head_ref, g).astype(jnp.bfloat16)
        cols = slice(g * HD, (g + 1) * HD)
        mains.append(dot(head, w_ref[0:HD, cols], NT))
        tails.append(dot(head, w_ref[PIECE - HD : PIECE, cols], NT))
    packed = jnp.concatenate(mains + [pack_tail(tails, 3)], axis=0).astype(jnp.bfloat16)
    for i in range(n):
        out_ref[i] = packed


def probs_kernel(len_ref, q_ref, k_ref, out_ref, bias_ref):
    rows = k_ref.shape[0]

    @pl.when(pl.program_id(0) == 0)
    def _():
        s = lax.broadcasted_iota(jnp.int32, (rows, rows), 0)
        t = lax.broadcasted_iota(jnp.int32, (rows, rows), 1)
        start = jnp.zeros((rows, rows), jnp.int32)
        end = 0
        for j in range(SEQ_DEV - 1):
            end = end + len_ref[0, j]
            start = jnp.where(t >= end, end, start)
        bias_ref[...] = jnp.where((s <= t) & (s >= start), 0.0, -jnp.inf)

    bias = bias_ref[...]
    scale = math.log2(math.e) / math.sqrt(HD)
    for p in range(QPK):
        score = dot(k_ref[...], q_ref[:, p * HD : (p + 1) * HD], NT) + bias
        top = jnp.max(score, axis=0, keepdims=True)
        expo = jnp.exp2((score - top) * scale)
        total = jnp.sum(expo, axis=0, keepdims=True)
        out_ref[p] = (expo * (1.0 / total)).astype(jnp.bfloat16)


def main_kernel(grad_scale, len_ref, wh_ref, x_ref, p_ref, target_ref, mask_ref, val_ref, out_ref, wht_ref, gt_ref):
    n = wh_ref.shape[0]
    rows = x_ref.shape[0]
    group32, group8 = lane_group(HROWS), lane_group(GR)
    for k in range(n // 4):
        main = [wh_ref[4 * k + r, 0:HROWS, :].astype(jnp.float32) for r in range(4)]
        tail = [wh_ref[4 * k + r, HROWS:PROWS, :].astype(jnp.float32) for r in range(4)]
        for q in range(5):
            tile = turn(main[q], TAIL * q) if q < 4 else None
            if q >= 1:
                r = q - 1
                tails = jnp.concatenate([turn(tail[r], TAIL * (r - g)) for g in range(KVH)], axis=0)
                tile = tails if tile is None else jnp.where(group32 >= q, tile, tails)
                if r >= 1:
                    tile = jnp.where(group32 < r, turn(main[r], TAIL * r), tile)
            j = 5 * k + q
            wht_ref[:, j * HD : (j + 1) * HD] = tile.astype(jnp.bfloat16)
    u = dot(wht_ref[...], x_ref[...], NT)
    u2 = jnp.concatenate(split(u), axis=0)
    row64 = lax.broadcasted_iota(jnp.int32, (2 * HROWS, rows), 0) % HROWS
    zero64 = jnp.zeros((2 * HROWS, rows), jnp.bfloat16)
    acc = jnp.zeros((2 * HROWS, rows), jnp.float32)
    for q in range(QH):
        own = (q // QPK) * GR + q % QPK
        acc = acc + dot(jnp.where(row64 == own, u2, zero64), p_ref[q], NN)
    values = jnp.sum(acc, axis=0, keepdims=True)
    val_ref[...] = values
    pos = lax.broadcasted_iota(jnp.int32, (1, rows), 1)
    row8 = lax.broadcasted_iota(jnp.int32, (GR, HD), 0)
    lane8 = lax.broadcasted_iota(jnp.int32, (GR, HD), 1)
    means = jnp.zeros((GR, HD), jnp.float32)
    begin = 0
    for j in range(SEQ_DEV):
        size = len_ref[0, j]
        hit = (pos >= begin) & (pos < begin + size)
        begin = begin + size
        total = jnp.sum(jnp.where(hit, values, 0.0), axis=1, keepdims=True)
        mean = jnp.broadcast_to(total, (GR, HD)) / size.astype(jnp.float32)
        high = mean.astype(jnp.bfloat16).astype(jnp.float32)
        middle = (mean - high).astype(jnp.bfloat16).astype(jnp.float32)
        low = mean - high - middle
        term = jnp.where(row8 == QPK, high, jnp.where(row8 == QPK + 1, middle, low))
        means = jnp.where((lane8 == j) & (row8 >= QPK), term, means)
    resid = jnp.where(mask_ref[...] == 1, values - target_ref[...], 0.0) * grad_scale
    r_high, r_low = split(resid)
    both = jnp.concatenate(
        [jnp.broadcast_to(r_high, (HROWS, rows)), jnp.broadcast_to(r_low, (HROWS, rows))], axis=0
    )
    acc = jnp.zeros((2 * HROWS, rows), jnp.float32)
    for q in range(QH):
        own = (q // QPK) * GR + q % QPK
        acc = acc + dot(jnp.where(row64 == own, both, zero64), p_ref[q], NT)
    c = acc[0:HROWS] + acc[HROWS:]
    g2 = dot(jnp.concatenate(split(c), axis=0), x_ref[...], NN)
    gt_ref[...] = g2[0:HROWS] + g2[HROWS:]
    for k in range(n // 4):
        tiles = [gt_ref[:, (5 * k + q) * HD : (5 * k + q + 1) * HD] for q in range(5)]
        for r in range(4):
            main = tiles[r]
            if r:
                main = jnp.where(group32 < 4 - r, turn(tiles[r], -TAIL * r), turn(tiles[r + 1], -TAIL * r))
            tail = pack_tail([tiles[r + 1][g * GR : (g + 1) * GR] for g in range(KVH)], r) + means
            out_ref[4 * k + r] = jnp.concatenate([main, tail], axis=0).astype(jnp.bfloat16)


def group_kernel(plan_ref, in_ref, seq_ref, out_ref):
    total = jnp.sum(in_ref[...].astype(jnp.float32), axis=0).astype(jnp.bfloat16)
    for i in range(out_ref.shape[0]):
        out_ref[i] = total
    row8 = lax.broadcasted_iota(jnp.int32, (GR, HD), 0)
    lane8 = lax.broadcasted_iota(jnp.int32, (GR, HD), 1)
    lane = lax.broadcasted_iota(jnp.int32, (1, SEQ_DEV), 1)
    out = jnp.zeros((1, SEQ_DEV), jnp.float32)
    for i in range(SEQ_DEV):
        slot = plan_ref[0, i]
        block = in_ref[lax.div(slot, SEQ_DEV), HROWS:PROWS, :].astype(jnp.float32)
        block = jnp.where((lane8 == lax.rem(slot, SEQ_DEV)) & (row8 >= QPK), block, 0.0)
        mean = jnp.sum(jnp.sum(block, axis=0, keepdims=True), axis=1, keepdims=True)
        out = jnp.where(lane == i, mean, out)
    seq_ref[...] = out


def weight_kernel(head_ref, in_ref, out_ref):
    total = jnp.sum(in_ref[...].astype(jnp.float32), axis=0)
    main = total[0:HROWS]
    tail = jnp.concatenate([turn(total[HROWS:PROWS], -TAIL * g) for g in range(KVH)], axis=0)
    main2 = jnp.concatenate(split(main), axis=0)
    tail2 = jnp.concatenate(split(tail), axis=0)
    for g in range(KVH):
        head = head_rows(head_ref, g).astype(jnp.bfloat16)
        blank = jnp.zeros((GR, HD), jnp.bfloat16)
        block = jnp.concatenate([head if i == g else blank for i in range(KVH)] * 2, axis=0)
        cols = slice(g * HD, (g + 1) * HD)
        out_ref[0:HD, cols] = dot(main2, block, TN).astype(jnp.bfloat16)
        out_ref[HD:PIECE, cols] = dot(tail2, block, TN)[0:TAIL].astype(jnp.bfloat16)


def whole(shape):
    return pl.BlockSpec(shape, lambda: (0,) * len(shape))


def local(hidden, queries, keys, value_weight, value_head, lengths, plan, targets, loss_mask):
    n = lax.axis_size("fsdp")
    groups = lax.axis_size("dp")
    rows, d = hidden.shape[1:]
    grad_scale = 1.0 / math.sqrt(rows * n * groups)
    bf16, f32 = jnp.bfloat16, jnp.float32
    smem = pl.BlockSpec(memory_space=pltpu.SMEM)
    head = value_head.reshape(1, QH * HD)
    own_lengths = lengths.reshape(1, SEQ_DEV)

    folded = pl.pallas_call(
        fold_kernel,
        out_shape=jax.ShapeDtypeStruct((n, PROWS, HD), bf16),
        compiler_params=VMEM,
        name="fold",
    )(value_weight, head)
    every = lax.all_to_all(folded, "fsdp", 0, 0)

    probs = pl.pallas_call(
        probs_kernel,
        grid=(KVH,),
        in_specs=[
            smem,
            pl.BlockSpec((rows, QPK * HD), lambda g: (0, g)),
            pl.BlockSpec((rows, HD), lambda g: (0, g)),
        ],
        out_specs=pl.BlockSpec((QPK, rows, rows), lambda g: (g, 0, 0)),
        out_shape=jax.ShapeDtypeStruct((QH, rows, rows), bf16),
        scratch_shapes=[pltpu.VMEM((rows, rows), f32)],
        compiler_params=VMEM,
        cost_estimate=pl.CostEstimate(
            flops=2 * QH * rows * rows * HD, bytes_accessed=6 * 2**20, transcendentals=QH * rows * rows
        ),
        name="probs",
    )(own_lengths, queries[0], keys[0])

    values, pieces = pl.pallas_call(
        functools.partial(main_kernel, grad_scale),
        in_specs=[smem] + [pl.BlockSpec(memory_space=pltpu.VMEM)] * 5,
        out_shape=[jax.ShapeDtypeStruct((1, rows), f32), jax.ShapeDtypeStruct((n, PROWS, HD), bf16)],
        scratch_shapes=[pltpu.VMEM((HROWS, d), bf16), pltpu.VMEM((HROWS, d), f32)],
        compiler_params=VMEM,
        name="main",
    )(own_lengths, every, hidden[0], probs, targets, loss_mask)
    terms = lax.all_to_all(pieces, "fsdp", 0, 0)

    seq_values, copies = pl.pallas_call(
        group_kernel,
        in_specs=[smem, pl.BlockSpec(memory_space=pltpu.VMEM)],
        out_shape=[jax.ShapeDtypeStruct((1, SEQ_DEV), f32), jax.ShapeDtypeStruct((groups, PROWS, HD), bf16)],
        compiler_params=VMEM,
        name="group",
    )(plan, terms)
    sums = lax.all_to_all(copies, "dp", 0, 0)

    d_weight = pl.pallas_call(
        weight_kernel,
        out_shape=jax.ShapeDtypeStruct(value_weight.shape, bf16),
        compiler_params=VMEM,
        name="weight",
    )(head, sums)
    return values, seq_values, d_weight


def solution(mesh):
    in_specs = (
        P("dp", "fsdp", None),
        P("dp", "fsdp", None),
        P("dp", "fsdp", None),
        P("fsdp", None),
        P(),
        P("dp", "fsdp", None),
        P("dp", "fsdp"),
        P("dp", "fsdp"),
        P("dp", "fsdp"),
    )
    out_specs = (P("dp", "fsdp"), P("dp", "fsdp"), P("fsdp", None))
    return jax.shard_map(local, mesh=mesh, in_specs=in_specs, out_specs=out_specs, check_vma=False)
```

time: 512 us -> 94.6 us (0.18)
  the two profiles are of different devices: /device:TPU:204 before, /device:TPU:1 now
where the time goes in v1:
time: 94.6 us; the launch traced here: 94.2 us
  blocking collectives  47.9 us (51%)
  starting transfers between devices  18.6 us (20%)
  Pallas kernels  12.2 us (13%)
  waiting for transfers between devices  8.56 us (9%)
  local copies, waits for them, and re-layouts  6.28 us (7%)
    all_to_all x1, blocking collectives, local(): terms = lax.all_to_all(pieces, 'fsdp', 0, 0)  24.9 us
    all_to_all x1, blocking collectives, local(): sums = lax.all_to_all(copies, 'dp', 0, 0)  22.9 us
    all_to_all x1, starting transfers between devices, local(): every = lax.all_to_all(folded, 'fsdp', 0, 0)  18.6 us
    all_to_all x1, waiting for transfers between devices, local(): every = lax.all_to_all(folded, 'fsdp', 0, 0)  8.56 us
    pallas_call x1, Pallas kernels, local(): pl.pallas_call(functools.partial(main_kernel, grad_scale), in_specs=[smem...  5.75 us
    unnamed x18, local copies, waits for them, and re-layouts  5.58 us
    pallas_call x1, Pallas kernels, local(): pl.pallas_call(probs_kernel, grid=(KVH,), in_specs=[smem, pl.BlockSpec((r...  3.3 us
  transfers between devices with their start and end apart: 1, of which 1 were waited for; matrix products, arithmetic and copies ran while one was open for 0% of the time, Pallas kernels for 4%

profile of v1, /device:TPU:1, one launch (start us, length us, event | category | flops | bytes accessed | tf_op | source)
XLA Modules:
  0.0 94.2 jit_solution(15289959799965360663)
XLA Ops:
  0.6 0.7 reshape.13.head_ref
  1.3 0.0 copy-start.3
  1.3 0.9 copy-done.3
  2.2 0.0 copy-start.5
  2.2 0.0 copy-start.6
  2.3 1.0 %fold.1 = bf16[32,40,128]{2,1,0:T(8,128)(2,1)} custom-call(bf16[160,512]{1,0:T(8,128)(2,1)S(1)} %copy-done.3, bf16[1,2560]{1,0:T(2,128)(2,1)S(1)} %reshape.13.head_ref), custom_call_target="tpu_custom_call" | custom-call | tf_op jit(solution)/shard_map/fold/pallas_call | solution.py:212
  3.3 18.6 %all-to-all-start = ((bf16[32,40,128]{2,1,0:T(8,128)(2,1)}), bf16[32,40,128]{2,1,0:T(8,128)(2,1)S(1)}, u32[]{:S(2)}, u32[]{:S(2)}) async-start(bf16[32,40,128]{2,1,0:T(8,128)(2,1)} %fold.1), calls=%async_computation | async-start | bytes 655360 | tf_op jit(solution)/shard_map/all_to_all | solution.py:218
  21.9 0.0 copy-start.1
  21.9 1.3 %copy-done.1 = bf16[1,256,2560]{2,1,0:T(8,128)(2,1)S(1)} copy-done((bf16[1,256,2560]{2,1,0:T(8,128)(2,1)S(1)}, bf16[1,256,2560]{2,1,0:T(8,128)(2,1)}, u32[]{:S(2)}) %copy-start.1) | copy-done | bytes 1310744
  23.2 0.9 %copy-done.2 = bf16[1,256,512]{2,1,0:T(8,128)(2,1)S(1)} copy-done((bf16[1,256,512]{2,1,0:T(8,128)(2,1)S(1)}, bf16[1,256,512]{2,1,0:T(8,128)(2,1)}, u32[]{:S(2)}) %copy-start.2) | copy-done | bytes 262168
  24.2 0.7 copy-done.4
  24.8 3.3 %probs.1.p_ref = bf16[20,256,256]{2,1,0:T(8,128)(2,1)S(1)} custom-call(s32[1,4]{1,0:T(1,128)S(1)} %bitcast.7, bf16[256,2560]{1,0:T(8,128)(2,1)S(1)} %bitcast.5, bf16[256,512]{1,0:T(8,128)(2,1)S(1)} %bitcast.6), custom_call_target="tpu_custom_call" | custom-call | flops 335544320 | bytes 6291456 | tf_op jit(solution)/shard_map/probs/pallas_call | solution.py:220
  28.1 8.6 %all-to-all-done.wh_ref = bf16[32,40,128]{2,1,0:T(8,128)(2,1)S(1)} async-done(((bf16[32,40,128]{2,1,0:T(8,128)(2,1)}), bf16[32,40,128]{2,1,0:T(8,128)(2,1)S(1)}, u32[]{:S(2)}, u32[]{:S(2)}) %all-to-all-start) | async-done | bytes 327712 | tf_op jit(solution)/shard_map/all_to_all | solution.py:218
  36.7 0.0 copy-done.5
  36.7 0.0 copy-done.6
  36.7 0.0 copy-done.7
  36.7 0.0 copy-start
  36.7 1.7 %copy-done = bf16[1,256,5120]{2,1,0:T(8,128)(2,1)S(1)} copy-done((bf16[1,256,5120]{2,1,0:T(8,128)(2,1)S(1)}, bf16[1,256,5120]{2,1,0:T(8,128)(2,1)}, u32[]{:S(2)}) %copy-start) | copy-done | bytes 2621464
  38.4 5.7 %main.1 = (f32[1,256]{1,0:T(1,128)}, bf16[32,40,128]{2,1,0:T(8,128)(2,1)S(1)}) custom-call(s32[1,4]{1,0:T(1,128)S(1)} %bitcast.8, bf16[32,40,128]{2,1,0:T(8,128)(2,1)S(1)} %all-to-all-done.wh_ref, bf16[256,5120]{1,0:T(8,128)(2,1)S(1)} %bitcast.4, bf16[20,256,256]{2,1,0:T(8,128)(2,1)S(1)} %probs.1.p_ref, f32[1,256]{1,0:T(1,128)S(1)} %copy-done.6, ...), custom_call_target="tpu_custom_call" | custom-call | tf_op jit(solution)/shard_map/main/pallas_call | solution.py:238
  44.2 24.9 %all_to_all.15.in_ref = bf16[32,40,128]{2,1,0:T(8,128)(2,1)S(1)} all-to-all(bf16[32,40,128]{2,1,0:T(8,128)(2,1)S(1)} %get-tuple-element.8), channel_id=1, replica_groups=mesh['fsdp'=32,'dp'=24] {'fsdp'}, dimensions={0} | all-to-all | bytes 655360 | tf_op jit(solution)/shard_map/all_to_all | solution.py:246
  69.1 0.0 copy-done.8
  69.1 1.2 %group.1 = (f32[1,4]{1,0:T(1,128)}, bf16[24,40,128]{2,1,0:T(8,128)(2,1)S(1)}) custom-call(s32[1,4]{1,0:T(1,128)S(1)} %copy-done.8, bf16[32,40,128]{2,1,0:T(8,128)(2,1)S(1)} %all_to_all.15.in_ref), custom_call_target="tpu_custom_call" | custom-call | tf_op jit(solution)/shard_map/group/pallas_call | solution.py:248
  70.3 22.9 %all_to_all.16.in_ref = bf16[24,40,128]{2,1,0:T(8,128)(2,1)S(1)} all-to-all(bf16[24,40,128]{2,1,0:T(8,128)(2,1)S(1)} %get-tuple-element.10), channel_id=1, replica_groups=mesh['fsdp'=32,'dp'=24] {'dp'}, dimensions={0} | all-to-all | bytes 491520 | tf_op jit(solution)/shard_map/all_to_all | solution.py:255
  93.2 1.0 %weight.1 = bf16[160,512]{1,0:T(8,128)(2,1)} custom-call(bf16[1,2560]{1,0:T(2,128)(2,1)S(1)} %reshape.13.head_ref, bf16[24,40,128]{2,1,0:T(8,128)(2,1)S(1)} %all_to_all.16.in_ref), custom_call_target="tpu_custom_call" | custom-call | tf_op jit(solution)/shard_map/weight/pallas_call | solution.py:257
  (4 shorter events, 0.0 us)
Async XLA Ops:
  1.3 0.9 copy-start.3
  2.2 34.4 %copy-start.5 = (s32[1,1,4]{2,1,0:T(1,128)S(1)}, s32[1,1,4]{2,1,0:T(1,128)}, u32[]{:S(2)}) copy-start(s32[1,1,4]{2,1,0:T(1,128)} %param.14) | copy-start | bytes 52
  2.2 34.4 %copy-start.6 = (f32[1,256]{1,0:T(1,128)S(1)}, f32[1,256]{1,0:T(1,128)}, u32[]{:S(2)}) copy-start(f32[1,256]{1,0:T(1,128)} %target_ref.1) | copy-start | bytes 3076
  2.3 34.4 %copy-start.7 = (s32[1,256]{1,0:T(1,128)S(1)}, s32[1,256]{1,0:T(1,128)}, u32[]{:S(2)}) copy-start(s32[1,256]{1,0:T(1,128)} %mask_ref.1) | copy-start | bytes 3076
  3.3 33.4 %all-to-all-start = ((bf16[32,40,128]{2,1,0:T(8,128)(2,1)}), bf16[32,40,128]{2,1,0:T(8,128)(2,1)S(1)}, u32[]{:S(2)}, u32[]{:S(2)}) async-start(bf16[32,40,128]{2,1,0:T(8,128)(2,1)} %fold.1), calls=%async_computation | async-start | bytes 655360 | tf_op jit(solution)/shard_map/all_to_all | solution.py:218
  21.9 1.3 %copy-start.1 = (bf16[1,256,2560]{2,1,0:T(8,128)(2,1)S(1)}, bf16[1,256,2560]{2,1,0:T(8,128)(2,1)}, u32[]{:S(2)}) copy-start(bf16[1,256,2560]{2,1,0:T(8,128)(2,1)} %param.10) | copy-start | bytes 3932164
  23.2 0.9 %copy-start.2 = (bf16[1,256,512]{2,1,0:T(8,128)(2,1)S(1)}, bf16[1,256,512]{2,1,0:T(8,128)(2,1)}, u32[]{:S(2)}) copy-start(bf16[1,256,512]{2,1,0:T(8,128)(2,1)} %param.11) | copy-start | bytes 786436
  24.2 0.7 copy-start.4
  36.7 1.7 %copy-start = (bf16[1,256,5120]{2,1,0:T(8,128)(2,1)S(1)}, bf16[1,256,5120]{2,1,0:T(8,128)(2,1)}, u32[]{:S(2)}) copy-start(bf16[1,256,5120]{2,1,0:T(8,128)(2,1)} %param.9) | copy-start | bytes 7864324
  38.4 30.7 %copy-start.8 = (s32[1,4]{1,0:T(1,128)S(1)}, s32[1,4]{1,0:T(1,128)}, u32[]{:S(2)}) copy-start(s32[1,4]{1,0:T(1,128)} %plan_ref.1) | copy-start | bytes 52

commit v2 on v1

--- a/solution.py
+++ b/solution.py
@@ -6,6 +6,7 @@
 from jax import lax
 from jax.experimental import pallas as pl
 from jax.experimental.pallas import tpu as pltpu
+from jax.sharding import Mesh
 from jax.sharding import PartitionSpec as P
 
 KVH = 4
@@ -13,6 +14,9 @@
 QH = KVH * QPK
 HD = 128
 SEQ_DEV = 4
+AXES = {"zh": 4, "x": 4, "core": 2, "y": 8, "zl": 3}
+FSDP = ("zh", "x", "core")
+DP = ("y", "zl")
 GR = 8
 HROWS = KVH * GR
 PIECE = 160
@@ -98,13 +102,21 @@
         out_ref[p] = (expo * (1.0 / total)).astype(jnp.bfloat16)
 
 
-def main_kernel(grad_scale, len_ref, wh_ref, x_ref, p_ref, target_ref, mask_ref, val_ref, out_ref, wht_ref, gt_ref):
-    n = wh_ref.shape[0]
+def main_kernel(grad_scale, len_ref, own_ref, other_ref, x_ref, p_ref, target_ref, mask_ref, val_ref, out_ref, wht_ref, gt_ref):
+    n = 2 * own_ref.shape[0]
+    across, depth = out_ref.shape[:2]
     rows = x_ref.shape[0]
-    group32, group8 = lane_group(HROWS), lane_group(GR)
+    group32 = lane_group(HROWS)
+    core = lax.axis_index("core")
+    place = (lax.axis_index("zh") * AXES["x"] + lax.axis_index("x")) * AXES["core"] + core
+
+    def piece(i, part):
+        own, other = own_ref[i // 2, part, :].astype(jnp.float32), other_ref[i // 2, part, :].astype(jnp.float32)
+        return jnp.where(core == i % 2, own, other)
+
     for k in range(n // 4):
-        main = [wh_ref[4 * k + r, 0:HROWS, :].astype(jnp.float32) for r in range(4)]
-        tail = [wh_ref[4 * k + r, HROWS:PROWS, :].astype(jnp.float32) for r in range(4)]
+        main = [piece(4 * k + r, slice(0, HROWS)) for r in range(4)]
+        tail = [piece(4 * k + r, slice(HROWS, PROWS)) for r in range(4)]
         for q in range(5):
             tile = turn(main[q], TAIL * q) if q < 4 else None
             if q >= 1:
@@ -140,7 +152,7 @@
         middle = (mean - high).astype(jnp.bfloat16).astype(jnp.float32)
         low = mean - high - middle
         term = jnp.where(row8 == QPK, high, jnp.where(row8 == QPK + 1, middle, low))
-        means = jnp.where((lane8 == j) & (row8 >= QPK), term, means)
+        means = jnp.where((lane8 == SEQ_DEV * place + j) & (row8 >= QPK), term, means)
     resid = jnp.where(mask_ref[...] == 1, values - target_ref[...], 0.0) * grad_scale
     r_high, r_low = split(resid)
     both = jnp.concatenate(
@@ -150,8 +162,8 @@
     for q in range(QH):
         own = (q // QPK) * GR + q % QPK
         acc = acc + dot(jnp.where(row64 == own, both, zero64), p_ref[q], NT)
-    c = acc[0:HROWS] + acc[HROWS:]
-    g2 = dot(jnp.concatenate(split(c), axis=0), x_ref[...], NN)
+    c2 = jnp.concatenate(split(acc[0:HROWS] + acc[HROWS:]), axis=0)
+    g2 = dot(c2, x_ref[...], NN)
     gt_ref[...] = g2[0:HROWS] + g2[HROWS:]
     for k in range(n // 4):
         tiles = [gt_ref[:, (5 * k + q) * HD : (5 * k + q + 1) * HD] for q in range(5)]
@@ -160,23 +172,34 @@
             if r:
                 main = jnp.where(group32 < 4 - r, turn(tiles[r], -TAIL * r), turn(tiles[r + 1], -TAIL * r))
             tail = pack_tail([tiles[r + 1][g * GR : (g + 1) * GR] for g in range(KVH)], r) + means
-            out_ref[4 * k + r] = jnp.concatenate([main, tail], axis=0).astype(jnp.bfloat16)
+            i = 4 * k + r
+            out_ref[i % across, i // across] = jnp.concatenate([main, tail], axis=0).astype(jnp.bfloat16)
+
+
+def line_kernel(in_ref, out_ref):
+    low = AXES["zl"]
+    for h in range(AXES["zh"]):
+        total = jnp.sum(in_ref[:, h].astype(jnp.float32), axis=0).astype(jnp.bfloat16)
+        for i in range(low):
+            out_ref[h * low + i] = total
 
 
 def group_kernel(plan_ref, in_ref, seq_ref, out_ref):
     total = jnp.sum(in_ref[...].astype(jnp.float32), axis=0).astype(jnp.bfloat16)
     for i in range(out_ref.shape[0]):
         out_ref[i] = total
+    mine = lax.axis_index("zl")
+    block = jnp.zeros((GR, HD), jnp.float32)
+    for h in range(AXES["zh"]):
+        block = block + in_ref[h * AXES["zl"] + mine, HROWS:PROWS, :].astype(jnp.float32)
     row8 = lax.broadcasted_iota(jnp.int32, (GR, HD), 0)
-    lane8 = lax.broadcasted_iota(jnp.int32, (GR, HD), 1)
+    mean = jnp.sum(jnp.where(row8 >= QPK, block, 0.0), axis=0, keepdims=True)
+    slot = lax.broadcasted_iota(jnp.int32, (1, HD), 1)
     lane = lax.broadcasted_iota(jnp.int32, (1, SEQ_DEV), 1)
     out = jnp.zeros((1, SEQ_DEV), jnp.float32)
     for i in range(SEQ_DEV):
-        slot = plan_ref[0, i]
-        block = in_ref[lax.div(slot, SEQ_DEV), HROWS:PROWS, :].astype(jnp.float32)
-        block = jnp.where((lane8 == lax.rem(slot, SEQ_DEV)) & (row8 >= QPK), block, 0.0)
-        mean = jnp.sum(jnp.sum(block, axis=0, keepdims=True), axis=1, keepdims=True)
-        out = jnp.where(lane == i, mean, out)
+        own = jnp.sum(jnp.where(slot == plan_ref[0, i], mean, 0.0), axis=1, keepdims=True)
+        out = jnp.where(lane == i, own, out)
     seq_ref[...] = out
 
 
@@ -195,28 +218,24 @@
         out_ref[HD:PIECE, cols] = dot(tail2, block, TN)[0:TAIL].astype(jnp.bfloat16)
 
 
-def whole(shape):
-    return pl.BlockSpec(shape, lambda: (0,) * len(shape))
-
-
 def local(hidden, queries, keys, value_weight, value_head, lengths, plan, targets, loss_mask):
-    n = lax.axis_size("fsdp")
-    groups = lax.axis_size("dp")
+    n = math.prod(AXES[a] for a in FSDP)
+    groups = math.prod(AXES[a] for a in DP)
     rows, d = hidden.shape[1:]
     grad_scale = 1.0 / math.sqrt(rows * n * groups)
     bf16, f32 = jnp.bfloat16, jnp.float32
     smem = pl.BlockSpec(memory_space=pltpu.SMEM)
+    vmem = pl.BlockSpec(memory_space=pltpu.VMEM)
     head = value_head.reshape(1, QH * HD)
     own_lengths = lengths.reshape(1, SEQ_DEV)
 
     folded = pl.pallas_call(
         fold_kernel,
-        out_shape=jax.ShapeDtypeStruct((n, PROWS, HD), bf16),
+        out_shape=jax.ShapeDtypeStruct((n // 2, PROWS, HD), bf16),
         compiler_params=VMEM,
         name="fold",
     )(value_weight, head)
-    every = lax.all_to_all(folded, "fsdp", 0, 0)
-
+    own_core = lax.all_to_all(folded, ("zh", "x"), 0, 0)
     probs = pl.pallas_call(
         probs_kernel,
         grid=(KVH,),
@@ -235,24 +254,38 @@
         name="probs",
     )(own_lengths, queries[0], keys[0])
 
+    own_core, probs = lax.optimization_barrier((own_core, probs))
+    other_core = lax.ppermute(own_core, "core", [(0, 1), (1, 0)])
+
     values, pieces = pl.pallas_call(
         functools.partial(main_kernel, grad_scale),
-        in_specs=[smem] + [pl.BlockSpec(memory_space=pltpu.VMEM)] * 5,
-        out_shape=[jax.ShapeDtypeStruct((1, rows), f32), jax.ShapeDtypeStruct((n, PROWS, HD), bf16)],
+        in_specs=[smem] + [vmem] * 6,
+        out_shape=[
+            jax.ShapeDtypeStruct((1, rows), f32),
+            jax.ShapeDtypeStruct((n // AXES["zh"], AXES["zh"], PROWS, HD), bf16),
+        ],
         scratch_shapes=[pltpu.VMEM((HROWS, d), bf16), pltpu.VMEM((HROWS, d), f32)],
         compiler_params=VMEM,
         name="main",
-    )(own_lengths, every, hidden[0], probs, targets, loss_mask)
-    terms = lax.all_to_all(pieces, "fsdp", 0, 0)
+    )(own_lengths, own_core, other_core, hidden[0], probs, targets, loss_mask)
+    terms = lax.all_to_all(pieces, ("x", "core"), 0, 0)
+
+    line = pl.pallas_call(
+        line_kernel,
+        out_shape=jax.ShapeDtypeStruct((AXES["zh"] * AXES["zl"], PROWS, HD), bf16),
+        compiler_params=VMEM,
+        name="line",
+    )(terms)
+    lines = lax.all_to_all(line, ("zh", "zl"), 0, 0)
 
     seq_values, copies = pl.pallas_call(
         group_kernel,
-        in_specs=[smem, pl.BlockSpec(memory_space=pltpu.VMEM)],
-        out_shape=[jax.ShapeDtypeStruct((1, SEQ_DEV), f32), jax.ShapeDtypeStruct((groups, PROWS, HD), bf16)],
+        in_specs=[smem, vmem],
+        out_shape=[jax.ShapeDtypeStruct((1, SEQ_DEV), f32), jax.ShapeDtypeStruct((AXES["y"], PROWS, HD), bf16)],
         compiler_params=VMEM,
         name="group",
-    )(plan, terms)
-    sums = lax.all_to_all(copies, "dp", 0, 0)
+    )(plan, lines)
+    sums = lax.all_to_all(copies, "y", 0, 0)
 
     d_weight = pl.pallas_call(
         weight_kernel,
@@ -264,16 +297,17 @@
 
 
 def solution(mesh):
+    fine = Mesh(mesh.devices.reshape(tuple(AXES.values())), tuple(AXES))
     in_specs = (
-        P("dp", "fsdp", None),
-        P("dp", "fsdp", None),
-        P("dp", "fsdp", None),
-        P("fsdp", None),
+        P(DP, FSDP, None),
+        P(DP, FSDP, None),
+        P(DP, FSDP, None),
+        P(FSDP, None),
         P(),
-        P("dp", "fsdp", None),
-        P("dp", "fsdp"),
-        P("dp", "fsdp"),
-        P("dp", "fsdp"),
+        P(DP, FSDP, None),
+        P(DP, FSDP),
+        P(DP, FSDP),
+        P(DP, FSDP),
     )
-    out_specs = (P("dp", "fsdp"), P("dp", "fsdp"), P("fsdp", None))
-    return jax.shard_map(local, mesh=mesh, in_specs=in_specs, out_specs=out_specs, check_vma=False)
+    out_specs = (P(DP, FSDP), P(DP, FSDP), P(FSDP, None))
+    return jax.shard_map(local, mesh=fine, in_specs=in_specs, out_specs=out_specs, check_vma=False)

time: 94.6 us -> 88.8 us (0.939)
  the two profiles are of different devices: /device:TPU:1 before, /device:TPU:2 now
where the time goes in v2:
time: 88.8 us; the launch traced here: 88.3 us
  blocking collectives  41.7 us (47%)
  starting transfers between devices  19.4 us (22%)
  Pallas kernels  12.2 us (14%)
  waiting for transfers between devices  8 us (9%)
  local copies, waits for them, and re-layouts  6.3 us (7%)
    all_to_all x1, starting transfers between devices, local(): own_core = lax.all_to_all(folded, ('zh', 'x'), 0, 0)  17.5 us
    all_to_all x1, blocking collectives, local(): sums = lax.all_to_all(copies, 'y', 0, 0)  15.4 us
    all_to_all x1, blocking collectives, local(): lines = lax.all_to_all(line, ('zh', 'zl'), 0, 0)  15.1 us
    all_to_all x1, blocking collectives, local(): terms = lax.all_to_all(pieces, ('x', 'core'), 0, 0)  11.2 us
    all_to_all x1, waiting for transfers between devices, local(): own_core = lax.all_to_all(folded, ('zh', 'x'), 0, 0)  6.64 us
    pallas_call x1, Pallas kernels, local(): pl.pallas_call(functools.partial(main_kernel, grad_scale), in_specs=[smem...  5.76 us
    unnamed x18, local copies, waits for them, and re-layouts  5.58 us
    pallas_call x1, Pallas kernels, local(): pl.pallas_call(probs_kernel, grid=(KVH,), in_specs=[smem, pl.BlockSpec((r...  3.3 us
  transfers between devices with their start and end apart: 2, of which 2 were waited for; matrix products, arithmetic and copies ran while one was open for 0% of the time, Pallas kernels for 4%

profile of v2, /device:TPU:2, one launch (start us, length us, event | category | flops | bytes accessed | tf_op | source)
XLA Modules:
  0.0 88.3 jit_solution(12096413939807152351)
XLA Ops:
  0.6 0.0 copy-start.5
  0.6 0.0 copy-start.7
  0.7 0.0 copy-start.6
  0.7 0.7 reshape.13.head_ref
  1.4 0.9 %copy-done.3 = bf16[160,512]{1,0:T(8,128)(2,1)S(1)} copy-done((bf16[160,512]{1,0:T(8,128)(2,1)S(1)}, bf16[160,512]{1,0:T(8,128)(2,1)}, u32[]{:S(2)}) %copy-start.3) | copy-done | bytes 163864
  2.3 1.0 %fold.1 = bf16[16,40,128]{2,1,0:T(8,128)(2,1)} custom-call(bf16[160,512]{1,0:T(8,128)(2,1)S(1)} %copy-done.3, bf16[1,2560]{1,0:T(2,128)(2,1)S(1)} %reshape.13.head_ref), custom_call_target="tpu_custom_call" | custom-call | tf_op jit(solution)/shard_map/fold/pallas_call | solution.py:232
  3.2 17.5 %all-to-all-start = ((bf16[16,40,128]{2,1,0:T(8,128)(2,1)}), bf16[16,40,128]{2,1,0:T(8,128)(2,1)S(1)}, u32[]{:S(2)}, u32[]{:S(2)}) async-start(bf16[16,40,128]{2,1,0:T(8,128)(2,1)} %fold.1), calls=%async_computation | async-start | bytes 327680 | tf_op jit(solution)/shard_map/all_to_all | solution.py:238
  20.8 1.3 %copy-done.1 = bf16[1,256,2560]{2,1,0:T(8,128)(2,1)S(1)} copy-done((bf16[1,256,2560]{2,1,0:T(8,128)(2,1)S(1)}, bf16[1,256,2560]{2,1,0:T(8,128)(2,1)}, u32[]{:S(2)}) %copy-start.1) | copy-done | bytes 1310744
  22.1 0.9 %copy-done.2 = bf16[1,256,512]{2,1,0:T(8,128)(2,1)S(1)} copy-done((bf16[1,256,512]{2,1,0:T(8,128)(2,1)S(1)}, bf16[1,256,512]{2,1,0:T(8,128)(2,1)}, u32[]{:S(2)}) %copy-start.2) | copy-done | bytes 262168
  23.0 0.7 copy-done.4
  23.7 3.3 %probs.1.p_ref = bf16[20,256,256]{2,1,0:T(8,128)(2,1)S(1)} custom-call(s32[1,4]{1,0:T(1,128)S(1)} %bitcast.7, bf16[256,2560]{1,0:T(8,128)(2,1)S(1)} %bitcast.5, bf16[256,512]{1,0:T(8,128)(2,1)S(1)} %bitcast.6), custom_call_target="tpu_custom_call" | custom-call | flops 335544320 | bytes 6291456 | tf_op jit(solution)/shard_map/probs/pallas_call | solution.py:239
  27.0 6.6 %all-to-all-done.own_ref = bf16[16,40,128]{2,1,0:T(8,128)(2,1)S(1)} async-done(((bf16[16,40,128]{2,1,0:T(8,128)(2,1)}), bf16[16,40,128]{2,1,0:T(8,128)(2,1)S(1)}, u32[]{:S(2)}, u32[]{:S(2)}) %all-to-all-start) | async-done | bytes 163872 | tf_op jit(solution)/shard_map/all_to_all | solution.py:238
  33.6 1.9 %collective-permute-start = (bf16[16,40,128]{2,1,0:T(8,128)(2,1)S(1)}, bf16[16,40,128]{2,1,0:T(8,128)(2,1)S(1)}, u32[]{:S(2)}, u32[]{:S(2)}) collective-permute-start(bf16[16,40,128]{2,1,0:T(8,128)(2,1)S(1)} %all-to-all-done.own_ref), channel_id=1, source_target_pairs={{0,24},{24,0},{1,25},{25,1},{2,26},{26,2},{3,27},{27,3},{4,28},{28... | collective-permute-start | bytes 491528 | tf_op jit(solution)/shard_map/ppermute | solution.py:258
  35.5 1.4 %collective-permute-done.other_ref = bf16[16,40,128]{2,1,0:T(8,128)(2,1)S(1)} collective-permute-done((bf16[16,40,128]{2,1,0:T(8,128)(2,1)S(1)}, bf16[16,40,128]{2,1,0:T(8,128)(2,1)S(1)}, u32[]{:S(2)}, u32[]{:S(2)}) %collective-permute-start) | collective-permute-done | bytes 163872 | tf_op jit(solution)/shard_map/ppermute | solution.py:258
  36.9 0.0 copy-done.5
  36.9 0.0 copy-start
  36.9 1.7 %copy-done = bf16[1,256,5120]{2,1,0:T(8,128)(2,1)S(1)} copy-done((bf16[1,256,5120]{2,1,0:T(8,128)(2,1)S(1)}, bf16[1,256,5120]{2,1,0:T(8,128)(2,1)}, u32[]{:S(2)}) %copy-start) | copy-done | bytes 2621464
  38.7 5.8 %main.1 = (f32[1,256]{1,0:T(1,128)}, bf16[8,4,40,128]{3,2,1,0:T(8,128)(2,1)S(1)}) custom-call(s32[1,4]{1,0:T(1,128)S(1)} %bitcast.8, bf16[16,40,128]{2,1,0:T(8,128)(2,1)S(1)} %all-to-all-done.own_ref, bf16[16,40,128]{2,1,0:T(8,128)(2,1)S(1)} %collective-permute-done.other_ref, bf16[256,5120]{1,0:T(8,128)(2,1)S(1)} %bitcast.4, ...), custom_call_target="tpu_custom_call" | custom-call | tf_op jit(solution)/shard_map/main/pallas_call | solution.py:260
  44.4 11.2 %all_to_all.20.in_ref = bf16[8,4,40,128]{3,2,1,0:T(8,128)(2,1)S(1)} all-to-all(bf16[8,4,40,128]{3,2,1,0:T(8,128)(2,1)S(1)} %get-tuple-element.12), channel_id=1, replica_groups=mesh['zh'=4,'x'=4,'core'=2,'y'=8,'zl'=3] {'x','core'}, dimensions={0} | all-to-all | bytes 655360 | tf_op jit(solution)/shard_map/all_to_all | solution.py:271
  55.6 15.1 %all_to_all.21.in_ref = bf16[12,40,128]{2,1,0:T(8,128)(2,1)S(1)} all-to-all(bf16[12,40,128]{2,1,0:T(8,128)(2,1)S(1)} %line.1), channel_id=1, replica_groups=mesh['zh'=4,'x'=4,'core'=2,'y'=8,'zl'=3] {'zh','zl'}, dimensions={0} | all-to-all | bytes 245760 | tf_op jit(solution)/shard_map/all_to_all | solution.py:279
  70.7 0.0 copy-done.8
  70.7 1.2 %group.1 = (f32[1,4]{1,0:T(1,128)}, bf16[8,40,128]{2,1,0:T(8,128)(2,1)S(1)}) custom-call(s32[1,4]{1,0:T(1,128)S(1)} %copy-done.8, bf16[12,40,128]{2,1,0:T(8,128)(2,1)S(1)} %all_to_all.21.in_ref), custom_call_target="tpu_custom_call" | custom-call | tf_op jit(solution)/shard_map/group/pallas_call | solution.py:281
  71.9 15.4 %all_to_all.22.in_ref = bf16[8,40,128]{2,1,0:T(8,128)(2,1)S(1)} all-to-all(bf16[8,40,128]{2,1,0:T(8,128)(2,1)S(1)} %get-tuple-element.14), channel_id=1, replica_groups=mesh['zh'=4,'x'=4,'core'=2,'y'=8,'zl'=3] {'y'}, dimensions={0} | all-to-all | bytes 163840 | tf_op jit(solution)/shard_map/all_to_all | solution.py:288
  87.3 1.0 %weight.1 = bf16[160,512]{1,0:T(8,128)(2,1)} custom-call(bf16[1,2560]{1,0:T(2,128)(2,1)S(1)} %reshape.13.head_ref, bf16[8,40,128]{2,1,0:T(8,128)(2,1)S(1)} %all_to_all.22.in_ref), custom_call_target="tpu_custom_call" | custom-call | tf_op jit(solution)/shard_map/weight/pallas_call | solution.py:290
  (8 shorter events, 0.1 us)
Async XLA Ops:
  0.6 36.3 %copy-start.5 = (s32[1,1,4]{2,1,0:T(1,128)S(1)}, s32[1,1,4]{2,1,0:T(1,128)}, u32[]{:S(2)}) copy-start(s32[1,1,4]{2,1,0:T(1,128)} %param.14) | copy-start | bytes 52
  0.6 36.3 %copy-start.7 = (s32[1,256]{1,0:T(1,128)S(1)}, s32[1,256]{1,0:T(1,128)}, u32[]{:S(2)}) copy-start(s32[1,256]{1,0:T(1,128)} %mask_ref.1) | copy-start | bytes 3076
  0.7 36.3 %copy-start.6 = (f32[1,256]{1,0:T(1,128)S(1)}, f32[1,256]{1,0:T(1,128)}, u32[]{:S(2)}) copy-start(f32[1,256]{1,0:T(1,128)} %target_ref.1) | copy-start | bytes 3076
  1.4 0.9 %copy-start.3 = (bf16[160,512]{1,0:T(8,128)(2,1)S(1)}, bf16[160,512]{1,0:T(8,128)(2,1)}, u32[]{:S(2)}) copy-start(bf16[160,512]{1,0:T(8,128)(2,1)} %w_ref.1) | copy-start | bytes 491524
  3.2 30.4 %all-to-all-start = ((bf16[16,40,128]{2,1,0:T(8,128)(2,1)}), bf16[16,40,128]{2,1,0:T(8,128)(2,1)S(1)}, u32[]{:S(2)}, u32[]{:S(2)}) async-start(bf16[16,40,128]{2,1,0:T(8,128)(2,1)} %fold.1), calls=%async_computation | async-start | bytes 327680 | tf_op jit(solution)/shard_map/all_to_all | solution.py:238
  20.8 1.3 %copy-start.1 = (bf16[1,256,2560]{2,1,0:T(8,128)(2,1)S(1)}, bf16[1,256,2560]{2,1,0:T(8,128)(2,1)}, u32[]{:S(2)}) copy-start(bf16[1,256,2560]{2,1,0:T(8,128)(2,1)} %param.10) | copy-start | bytes 3932164
  22.1 0.9 %copy-start.2 = (bf16[1,256,512]{2,1,0:T(8,128)(2,1)S(1)}, bf16[1,256,512]{2,1,0:T(8,128)(2,1)}, u32[]{:S(2)}) copy-start(bf16[1,256,512]{2,1,0:T(8,128)(2,1)} %param.11) | copy-start | bytes 786436
  23.0 0.7 copy-start.4
  33.6 3.3 %collective-permute-start = (bf16[16,40,128]{2,1,0:T(8,128)(2,1)S(1)}, bf16[16,40,128]{2,1,0:T(8,128)(2,1)S(1)}, u32[]{:S(2)}, u32[]{:S(2)}) collective-permute-start(bf16[16,40,128]{2,1,0:T(8,128)(2,1)S(1)} %all-to-all-done.own_ref), channel_id=1, source_target_pairs={{0,24},{24,0},{1,25},{25,1},{2,26},{26,2},{3,27},{27,3},{4,28},{28... | collective-permute-start | bytes 491528 | tf_op jit(solution)/shard_map/ppermute | solution.py:258
  36.9 1.7 %copy-start = (bf16[1,256,5120]{2,1,0:T(8,128)(2,1)S(1)}, bf16[1,256,5120]{2,1,0:T(8,128)(2,1)}, u32[]{:S(2)}) copy-start(bf16[1,256,5120]{2,1,0:T(8,128)(2,1)} %param.9) | copy-start | bytes 7864324
  38.7 32.0 %copy-start.8 = (s32[1,4]{1,0:T(1,128)S(1)}, s32[1,4]{1,0:T(1,128)}, u32[]{:S(2)}) copy-start(s32[1,4]{1,0:T(1,128)} %plan_ref.1) | copy-start | bytes 52

commit v3 on v2

--- a/solution.py
+++ b/solution.py
@@ -27,6 +27,7 @@
 NN = (((1,), (0,)), ((), ()))
 TN = (((0,), (0,)), ((), ()))
 VMEM = pltpu.CompilerParams(vmem_limit_bytes=24 * 1024 * 1024)
+WIDE = pltpu.CompilerParams(vmem_limit_bytes=60 * 1024 * 1024)
 
 
 def dot(a, b, dims):
@@ -52,7 +53,7 @@
     out = jnp.zeros((GR, HD), jnp.float32)
     for p in range(QPK):
         q = g * QPK + p
-        line = head_ref[0:1, q * HD : (q + 1) * HD].astype(jnp.float32)
+        line = head_ref[q * HD : (q + 1) * HD].astype(jnp.float32).reshape(1, HD)
         out = jnp.where(row == p, jnp.broadcast_to(line, (GR, HD)), out)
     return out
 
@@ -78,7 +79,7 @@
         out_ref[i] = packed
 
 
-def probs_kernel(len_ref, q_ref, k_ref, out_ref, bias_ref):
+def probs_kernel(len_ref, q_ref, k_ref, out_ref, share_ref, bias_ref):
     rows = k_ref.shape[0]
 
     @pl.when(pl.program_id(0) == 0)
@@ -91,6 +92,16 @@
             end = end + len_ref[0, j]
             start = jnp.where(t >= end, end, start)
         bias_ref[...] = jnp.where((s <= t) & (s >= start), 0.0, -jnp.inf)
+        row = lax.broadcasted_iota(jnp.int32, (GR, rows), 0)
+        pos = lax.broadcasted_iota(jnp.int32, (GR, rows), 1)
+        share = jnp.zeros((GR, rows), jnp.float32)
+        begin = 0
+        for j in range(SEQ_DEV):
+            size = len_ref[0, j]
+            hit = (row == j) & (pos >= begin) & (pos < begin + size)
+            share = jnp.where(hit, 1.0 / (jnp.zeros((GR, rows), jnp.float32) + size.astype(jnp.float32)), share)
+            begin = begin + size
+        share_ref[...] = share
 
     bias = bias_ref[...]
     scale = math.log2(math.e) / math.sqrt(HD)
@@ -102,7 +113,9 @@
         out_ref[p] = (expo * (1.0 / total)).astype(jnp.bfloat16)
 
 
-def main_kernel(grad_scale, len_ref, own_ref, other_ref, x_ref, p_ref, target_ref, mask_ref, val_ref, out_ref, wht_ref, gt_ref):
+def main_kernel(
+    grad_scale, seen_ref, share_ref, own_ref, other_ref, x_ref, p_ref, target_ref, mask_ref, val_ref, out_ref, wht_ref, gt_ref
+):
     n = 2 * own_ref.shape[0]
     across, depth = out_ref.shape[:2]
     rows = x_ref.shape[0]
@@ -137,17 +150,12 @@
         acc = acc + dot(jnp.where(row64 == own, u2, zero64), p_ref[q], NN)
     values = jnp.sum(acc, axis=0, keepdims=True)
     val_ref[...] = values
-    pos = lax.broadcasted_iota(jnp.int32, (1, rows), 1)
     row8 = lax.broadcasted_iota(jnp.int32, (GR, HD), 0)
     lane8 = lax.broadcasted_iota(jnp.int32, (GR, HD), 1)
     means = jnp.zeros((GR, HD), jnp.float32)
-    begin = 0
     for j in range(SEQ_DEV):
-        size = len_ref[0, j]
-        hit = (pos >= begin) & (pos < begin + size)
-        begin = begin + size
-        total = jnp.sum(jnp.where(hit, values, 0.0), axis=1, keepdims=True)
-        mean = jnp.broadcast_to(total, (GR, HD)) / size.astype(jnp.float32)
+        total = jnp.sum(share_ref[j : j + 1, :] * values, axis=1, keepdims=True)
+        mean = jnp.broadcast_to(total, (GR, HD))
         high = mean.astype(jnp.bfloat16).astype(jnp.float32)
         middle = (mean - high).astype(jnp.bfloat16).astype(jnp.float32)
         low = mean - high - middle
@@ -176,6 +184,10 @@
             out_ref[i % across, i // across] = jnp.concatenate([main, tail], axis=0).astype(jnp.bfloat16)
 
 
+def seen_kernel(x_ref, own_ref, out_ref):
+    out_ref[...] = x_ref[0:GR, 0:HD].astype(jnp.float32)
+
+
 def line_kernel(in_ref, out_ref):
     low = AXES["zl"]
     for h in range(AXES["zh"]):
@@ -184,10 +196,14 @@
             out_ref[h * low + i] = total
 
 
-def group_kernel(plan_ref, in_ref, seq_ref, out_ref):
+def group_kernel(in_ref, out_ref):
     total = jnp.sum(in_ref[...].astype(jnp.float32), axis=0).astype(jnp.bfloat16)
     for i in range(out_ref.shape[0]):
         out_ref[i] = total
+
+
+def seq_kernel(plan_ref, in_ref, own_ref, seq_ref, val_ref):
+    val_ref[...] = own_ref[...]
     mine = lax.axis_index("zl")
     block = jnp.zeros((GR, HD), jnp.float32)
     for h in range(AXES["zh"]):
@@ -226,17 +242,16 @@
     bf16, f32 = jnp.bfloat16, jnp.float32
     smem = pl.BlockSpec(memory_space=pltpu.SMEM)
     vmem = pl.BlockSpec(memory_space=pltpu.VMEM)
-    head = value_head.reshape(1, QH * HD)
     own_lengths = lengths.reshape(1, SEQ_DEV)
 
     folded = pl.pallas_call(
         fold_kernel,
         out_shape=jax.ShapeDtypeStruct((n // 2, PROWS, HD), bf16),
-        compiler_params=VMEM,
+        compiler_params=WIDE,
         name="fold",
-    )(value_weight, head)
+    )(value_weight, value_head)
     own_core = lax.all_to_all(folded, ("zh", "x"), 0, 0)
-    probs = pl.pallas_call(
+    probs, share = pl.pallas_call(
         probs_kernel,
         grid=(KVH,),
         in_specs=[
@@ -244,10 +259,13 @@
             pl.BlockSpec((rows, QPK * HD), lambda g: (0, g)),
             pl.BlockSpec((rows, HD), lambda g: (0, g)),
         ],
-        out_specs=pl.BlockSpec((QPK, rows, rows), lambda g: (g, 0, 0)),
-        out_shape=jax.ShapeDtypeStruct((QH, rows, rows), bf16),
+        out_specs=[
+            pl.BlockSpec((QPK, rows, rows), lambda g: (g, 0, 0)),
+            pl.BlockSpec((GR, rows), lambda g: (0, 0)),
+        ],
+        out_shape=[jax.ShapeDtypeStruct((QH, rows, rows), bf16), jax.ShapeDtypeStruct((GR, rows), f32)],
         scratch_shapes=[pltpu.VMEM((rows, rows), f32)],
-        compiler_params=VMEM,
+        compiler_params=WIDE,
         cost_estimate=pl.CostEstimate(
             flops=2 * QH * rows * rows * HD, bytes_accessed=6 * 2**20, transcendentals=QH * rows * rows
         ),
@@ -257,9 +275,18 @@
     own_core, probs = lax.optimization_barrier((own_core, probs))
     other_core = lax.ppermute(own_core, "core", [(0, 1), (1, 0)])
 
-    values, pieces = pl.pallas_call(
+    seen = pl.pallas_call(
+        seen_kernel,
+        in_specs=[vmem, pl.BlockSpec(memory_space=pl.ANY)],
+        out_shape=jax.ShapeDtypeStruct((GR, HD), f32),
+        compiler_params=VMEM,
+        cost_estimate=pl.CostEstimate(flops=0, bytes_accessed=4 * 2**20, transcendentals=0),
+        name="seen",
+    )(hidden[0], own_core)
+
+    own_values, pieces = pl.pallas_call(
         functools.partial(main_kernel, grad_scale),
-        in_specs=[smem] + [vmem] * 6,
+        in_specs=[pl.BlockSpec(memory_space=pl.ANY)] + [vmem] * 7,
         out_shape=[
             jax.ShapeDtypeStruct((1, rows), f32),
             jax.ShapeDtypeStruct((n // AXES["zh"], AXES["zh"], PROWS, HD), bf16),
@@ -267,7 +294,7 @@
         scratch_shapes=[pltpu.VMEM((HROWS, d), bf16), pltpu.VMEM((HROWS, d), f32)],
         compiler_params=VMEM,
         name="main",
-    )(own_lengths, own_core, other_core, hidden[0], probs, targets, loss_mask)
+    )(seen, share, own_core, other_core, hidden[0], probs, targets, loss_mask)
     terms = lax.all_to_all(pieces, ("x", "core"), 0, 0)
 
     line = pl.pallas_call(
@@ -278,21 +305,29 @@
     )(terms)
     lines = lax.all_to_all(line, ("zh", "zl"), 0, 0)
 
-    seq_values, copies = pl.pallas_call(
+    copies = pl.pallas_call(
         group_kernel,
-        in_specs=[smem, vmem],
-        out_shape=[jax.ShapeDtypeStruct((1, SEQ_DEV), f32), jax.ShapeDtypeStruct((AXES["y"], PROWS, HD), bf16)],
+        out_shape=jax.ShapeDtypeStruct((AXES["y"], PROWS, HD), bf16),
         compiler_params=VMEM,
         name="group",
-    )(plan, lines)
+    )(lines)
     sums = lax.all_to_all(copies, "y", 0, 0)
+
+    seq_values, values = pl.pallas_call(
+        seq_kernel,
+        in_specs=[smem, vmem, vmem],
+        out_shape=[jax.ShapeDtypeStruct((1, SEQ_DEV), f32), jax.ShapeDtypeStruct((1, rows), f32)],
+        compiler_params=VMEM,
+        cost_estimate=pl.CostEstimate(flops=2**20, bytes_accessed=2**20, transcendentals=0),
+        name="seq",
+    )(plan, lines, own_values)
 
     d_weight = pl.pallas_call(
         weight_kernel,
         out_shape=jax.ShapeDtypeStruct(value_weight.shape, bf16),
         compiler_params=VMEM,
         name="weight",
-    )(head, sums)
+    )(value_head, sums)
     return values, seq_values, d_weight
 
 

time: 88.8 us -> 85.4 us (0.962)
  blocking collectives: 41.7 us -> 26.2 us
  waiting for transfers between devices: 8 us -> 16.5 us
  starting transfers between devices: 19.4 us -> 26.8 us
  local copies, waits for them, and re-layouts: 6.3 us -> 0.03 us
  Pallas kernels: 12.2 us -> 14.6 us
    all_to_all x1 -> x0, blocking collectives: 15.4 us -> none  [local(): sums = lax.all_to_all(copies, 'y', 0, 0)]
    all_to_all x0 -> x1, waiting for transfers between devices: none -> 7.39 us  [local(): sums = lax.all_to_all(copies, 'y', 0, 0)]
    all_to_all x0 -> x1, starting transfers between devices: none -> 7.1 us  [local(): sums = lax.all_to_all(copies, 'y', 0, 0)]
    unnamed x18 -> x14, local copies, waits for them, and re-layouts: 5.58 us -> 0.03 us
    pallas_call x1, Pallas kernels: 3.3 us -> 5.04 us  [local(): pl.pallas_call(probs_kernel, grid=(KVH,), in_specs=[smem, pl.BlockSpec((r...]
    all_to_all x1, waiting for transfers between devices: 6.64 us -> 7.8 us  [local(): own_core = lax.all_to_all(folded, ('zh', 'x'), 0, 0)]
    pallas_call x1, Pallas kernels: 0.95 us -> 2.02 us  [local(): pl.pallas_call(fold_kernel, out_shape=jax.ShapeDtypeStruct((n // 2, PROWS...]
    pallas_call x2 -> x4, Pallas kernels: 6.92 us -> 6.55 us  [the longest x1 4.73 us: local(): pl.pallas_call(functools.partial(main_kernel, grad_scale), in_specs=[pl.B...]
  transfers between devices with their start and end apart: 2 -> 3, of which waited for: 2 -> 3; matrix products, arithmetic and copies ran while one was open for 0% -> 0% of each run, Pallas kernels for 4% -> 7%
where the time goes in v3:
time: 85.4 us; the launch traced here: 85 us
  starting transfers between devices  26.8 us (31%)
  blocking collectives  26.2 us (31%)
  waiting for transfers between devices  16.5 us (19%)
  Pallas kernels  14.6 us (17%)
    all_to_all x1, starting transfers between devices, local(): own_core = lax.all_to_all(folded, ('zh', 'x'), 0, 0)  17.5 us
    all_to_all x1, blocking collectives, local(): lines = lax.all_to_all(line, ('zh', 'zl'), 0, 0)  15.1 us
    all_to_all x1, blocking collectives, local(): terms = lax.all_to_all(pieces, ('x', 'core'), 0, 0)  11.2 us
    all_to_all x1, waiting for transfers between devices, local(): own_core = lax.all_to_all(folded, ('zh', 'x'), 0, 0)  7.8 us
    all_to_all x1, waiting for transfers between devices, local(): sums = lax.all_to_all(copies, 'y', 0, 0)  7.39 us
    all_to_all x1, starting transfers between devices, local(): sums = lax.all_to_all(copies, 'y', 0, 0)  7.1 us
    pallas_call x1, Pallas kernels, local(): pl.pallas_call(probs_kernel, grid=(KVH,), in_specs=[smem, pl.BlockSpec((r...  5.04 us
    pallas_call x1, Pallas kernels, local(): pl.pallas_call(functools.partial(main_kernel, grad_scale), in_specs=[pl.B...  4.73 us
  transfers between devices with their start and end apart: 3, of which 3 were waited for; matrix products, arithmetic and copies ran while one was open for 0% of the time, Pallas kernels for 7%

profile of v3, /device:TPU:2, one launch (start us, length us, event | category | flops | bytes accessed | tf_op | source)
XLA Modules:
  0.0 85.0 jit_solution(2451822840037409193)
XLA Ops:
  0.6 0.0 copy-start
  0.6 2.0 %fold.1 = bf16[16,40,128]{2,1,0:T(8,128)(2,1)} custom-call(bf16[160,512]{1,0:T(8,128)(2,1)} %w_ref.1, bf16[2560]{0:T(1024)(128)(2,1)} %head_ref.3), custom_call_target="tpu_custom_call" | custom-call | tf_op jit(solution)/shard_map/fold/pallas_call | solution.py:247
  2.7 17.5 %all-to-all-start = ((bf16[16,40,128]{2,1,0:T(8,128)(2,1)}), bf16[16,40,128]{2,1,0:T(8,128)(2,1)S(1)}, u32[]{:S(2)}, u32[]{:S(2)}) async-start(bf16[16,40,128]{2,1,0:T(8,128)(2,1)} %fold.1), calls=%async_computation | async-start | bytes 327680 | tf_op jit(solution)/shard_map/all_to_all | solution.py:253
  20.2 0.0 copy-start.5
  20.2 5.0 %probs.1 = (bf16[20,256,256]{2,1,0:T(8,128)(2,1)}, f32[8,256]{1,0:T(8,128)}) custom-call(s32[1,4]{1,0:T(1,128)} %bitcast.8, bf16[256,2560]{1,0:T(8,128)(2,1)} %bitcast.6, bf16[256,512]{1,0:T(8,128)(2,1)} %bitcast.7), custom_call_target="tpu_custom_call" | custom-call | flops 335544320 | bytes 6291456 | tf_op jit(solution)/shard_map/probs/pallas_call | solution.py:254
  25.2 7.8 %all-to-all-done.own_ref = bf16[16,40,128]{2,1,0:T(8,128)(2,1)S(1)} async-done(((bf16[16,40,128]{2,1,0:T(8,128)(2,1)}), bf16[16,40,128]{2,1,0:T(8,128)(2,1)S(1)}, u32[]{:S(2)}, u32[]{:S(2)}) %all-to-all-start) | async-done | bytes 163872 | tf_op jit(solution)/shard_map/all_to_all | solution.py:253
  33.0 2.2 %collective-permute-start = (bf16[16,40,128]{2,1,0:T(8,128)(2,1)S(1)}, bf16[16,40,128]{2,1,0:T(8,128)(2,1)S(1)}, u32[]{:S(2)}, u32[]{:S(2)}) collective-permute-start(bf16[16,40,128]{2,1,0:T(8,128)(2,1)S(1)} %all-to-all-done.own_ref), channel_id=1, source_target_pairs={{0,24},{24,0},{1,25},{25,1},{2,26},{26,2},{3,27},{27,3},{4,28},{28... | collective-permute-start | bytes 491528 | tf_op jit(solution)/shard_map/ppermute | solution.py:276
  35.2 0.0 copy-done
  35.2 1.3 %collective-permute-done.other_ref = bf16[16,40,128]{2,1,0:T(8,128)(2,1)S(1)} collective-permute-done((bf16[16,40,128]{2,1,0:T(8,128)(2,1)S(1)}, bf16[16,40,128]{2,1,0:T(8,128)(2,1)S(1)}, u32[]{:S(2)}, u32[]{:S(2)}) %collective-permute-start) | collective-permute-done | bytes 163872 | tf_op jit(solution)/shard_map/ppermute | solution.py:276
  36.6 0.0 copy-done.4
  36.6 0.0 copy-done.5
  36.6 0.0 copy-done.3
  36.6 0.0 copy-done.1
  36.6 0.0 copy-start.6
  36.6 0.0 copy-start.2
  36.6 4.7 %main.1 = (f32[1,256]{1,0:T(1,128)S(1)}, bf16[8,4,40,128]{3,2,1,0:T(8,128)(2,1)S(1)}) custom-call(f32[8,128]{1,0:T(8,128)S(1)} %seen.1.seen_ref, f32[8,256]{1,0:T(8,128)S(1)} %copy-done.3, bf16[16,40,128]{2,1,0:T(8,128)(2,1)S(1)} %all-to-all-done.own_ref, bf16[16,40,128]{2,1,0:T(8,128)(2,1)S(1)} %collective-permute-done.other_ref, ...), custom_call_target="tpu_custom_call" | custom-call | tf_op jit(solution)/shard_map/main/pallas_call | solution.py:287
  41.4 11.2 %all_to_all.20.in_ref = bf16[8,4,40,128]{3,2,1,0:T(8,128)(2,1)S(1)} all-to-all(bf16[8,4,40,128]{3,2,1,0:T(8,128)(2,1)S(1)} %get-tuple-element.15), channel_id=1, replica_groups=mesh['zh'=4,'x'=4,'core'=2,'y'=8,'zl'=3] {'x','core'}, dimensions={0} | all-to-all | bytes 655360 | tf_op jit(solution)/shard_map/all_to_all | solution.py:298
  52.6 15.1 %all_to_all.21.in_ref = bf16[12,40,128]{2,1,0:T(8,128)(2,1)S(1)} all-to-all(bf16[12,40,128]{2,1,0:T(8,128)(2,1)S(1)} %line.1), channel_id=1, replica_groups=mesh['zh'=4,'x'=4,'core'=2,'y'=8,'zl'=3] {'zh','zl'}, dimensions={0} | all-to-all | bytes 245760 | tf_op jit(solution)/shard_map/all_to_all | solution.py:306
  67.7 0.7 group.1
  68.3 7.1 %all-to-all-start.3 = ((bf16[8,40,128]{2,1,0:T(8,128)(2,1)}), bf16[8,40,128]{2,1,0:T(8,128)(2,1)S(1)}, u32[]{:S(2)}, u32[]{:S(2)}) async-start(bf16[8,40,128]{2,1,0:T(8,128)(2,1)} %group.1), calls=%async_computation.3 | async-start | bytes 163840 | tf_op jit(solution)/shard_map/all_to_all | solution.py:314
  75.4 0.0 copy-done.6
  75.4 1.2 %seq.1 = (f32[1,4]{1,0:T(1,128)}, f32[1,256]{1,0:T(1,128)}) custom-call(s32[1,4]{1,0:T(1,128)S(1)} %copy-done.6, bf16[12,40,128]{2,1,0:T(8,128)(2,1)S(1)} %all_to_all.21.in_ref, f32[1,256]{1,0:T(1,128)S(1)} %get-tuple-element.16.own_ref), custom_call_target="tpu_custom_call" | custom-call | flops 1048576 | bytes 1048576 | tf_op jit(solution)/shard_map/seq/pallas_call | solution.py:316
  76.6 7.4 %all-to-all-done.3.in_ref = bf16[8,40,128]{2,1,0:T(8,128)(2,1)S(1)} async-done(((bf16[8,40,128]{2,1,0:T(8,128)(2,1)}), bf16[8,40,128]{2,1,0:T(8,128)(2,1)S(1)}, u32[]{:S(2)}, u32[]{:S(2)}) %all-to-all-start.3) | async-done | bytes 81952 | tf_op jit(solution)/shard_map/all_to_all | solution.py:314
  84.0 1.0 %weight.1 = bf16[160,512]{1,0:T(8,128)(2,1)} custom-call(bf16[2560]{0:T(1024)(128)(2,1)S(1)} %copy-done.2, bf16[8,40,128]{2,1,0:T(8,128)(2,1)S(1)} %all-to-all-done.3.in_ref), custom_call_target="tpu_custom_call" | custom-call | tf_op jit(solution)/shard_map/weight/pallas_call | solution.py:325
  (6 shorter events, 0.1 us)
Async XLA Ops:
  0.6 34.6 %copy-start = (bf16[1,256,5120]{2,1,0:T(8,128)(2,1)S(1)}, bf16[1,256,5120]{2,1,0:T(8,128)(2,1)}, u32[]{:S(2)}) copy-start(bf16[1,256,5120]{2,1,0:T(8,128)(2,1)} %param.9) | copy-start | bytes 7864324
  2.7 30.4 %all-to-all-start = ((bf16[16,40,128]{2,1,0:T(8,128)(2,1)}), bf16[16,40,128]{2,1,0:T(8,128)(2,1)S(1)}, u32[]{:S(2)}, u32[]{:S(2)}) async-start(bf16[16,40,128]{2,1,0:T(8,128)(2,1)} %fold.1), calls=%async_computation | async-start | bytes 327680 | tf_op jit(solution)/shard_map/all_to_all | solution.py:253
  20.2 16.4 %copy-start.4 = (f32[1,256]{1,0:T(1,128)S(1)}, f32[1,256]{1,0:T(1,128)}, u32[]{:S(2)}) copy-start(f32[1,256]{1,0:T(1,128)} %target_ref.1) | copy-start | bytes 3076
  20.2 16.4 %copy-start.5 = (s32[1,256]{1,0:T(1,128)S(1)}, s32[1,256]{1,0:T(1,128)}, u32[]{:S(2)}) copy-start(s32[1,256]{1,0:T(1,128)} %mask_ref.1) | copy-start | bytes 3076
  25.2 11.4 %copy-start.3 = (f32[8,256]{1,0:T(8,128)S(1)}, f32[8,256]{1,0:T(8,128)}, u32[]{:S(2)}) copy-start(f32[8,256]{1,0:T(8,128)} %get-tuple-element.13.share_ref) | copy-start | bytes 24580
  33.0 3.6 %copy-start.1 = (bf16[20,256,256]{2,1,0:T(8,128)(2,1)S(1)}, bf16[20,256,256]{2,1,0:T(8,128)(2,1)}, u32[]{:S(2)}) copy-start(bf16[20,256,256]{2,1,0:T(8,128)(2,1)} %get-tuple-element.14.p_ref) | copy-start | bytes 7864324
  33.0 3.5 %collective-permute-start = (bf16[16,40,128]{2,1,0:T(8,128)(2,1)S(1)}, bf16[16,40,128]{2,1,0:T(8,128)(2,1)S(1)}, u32[]{:S(2)}, u32[]{:S(2)}) collective-permute-start(bf16[16,40,128]{2,1,0:T(8,128)(2,1)S(1)} %all-to-all-done.own_ref), channel_id=1, source_target_pairs={{0,24},{24,0},{1,25},{25,1},{2,26},{26,2},{3,27},{27,3},{4,28},{28... | collective-permute-start | bytes 491528 | tf_op jit(solution)/shard_map/ppermute | solution.py:276
  36.6 38.8 %copy-start.6 = (s32[1,4]{1,0:T(1,128)S(1)}, s32[1,4]{1,0:T(1,128)}, u32[]{:S(2)}) copy-start(s32[1,4]{1,0:T(1,128)} %plan_ref.1) | copy-start | bytes 52
  36.6 47.4 %copy-start.2 = (bf16[2560]{0:T(1024)(128)(2,1)S(1)}, bf16[2560]{0:T(1024)(128)(2,1)}, u32[]{:S(2)}) copy-start(bf16[2560]{0:T(1024)(128)(2,1)} %head_ref.3) | copy-start | bytes 15364
  68.3 15.7 %all-to-all-start.3 = ((bf16[8,40,128]{2,1,0:T(8,128)(2,1)}), bf16[8,40,128]{2,1,0:T(8,128)(2,1)S(1)}, u32[]{:S(2)}, u32[]{:S(2)}) async-start(bf16[8,40,128]{2,1,0:T(8,128)(2,1)} %group.1), calls=%async_computation.3 | async-start | bytes 163840 | tf_op jit(solution)/shard_map/all_to_all | solution.py:314

commit v4 on v3

--- a/solution.py
+++ b/solution.py
@@ -18,9 +18,10 @@
 FSDP = ("zh", "x", "core")
 DP = ("y", "zl")
 GR = 8
-HROWS = KVH * GR
+QR = 24
 PIECE = 160
-PROWS = HROWS + 8
+PROWS = QR + GR
+BOTH = QR + KVH * GR
 TAIL = 32
 
 NT = (((1,), (1,)), ((), ()))
@@ -34,9 +35,9 @@
     return lax.dot_general(a, b, dims, preferred_element_type=jnp.float32)
 
 
-def split(x):
-    high = x.astype(jnp.bfloat16)
-    return high, (x - high.astype(jnp.float32)).astype(jnp.bfloat16)
+def two_terms(x):
+    high = x.astype(jnp.bfloat16).astype(jnp.float32)
+    return jnp.concatenate([high, x - high], axis=0).astype(jnp.bfloat16)
 
 
 def lane_group(rows):
@@ -48,14 +49,19 @@
     return x if shift == 0 else pltpu.roll(x, shift, 1)
 
 
-def head_rows(head_ref, g):
-    row = lax.broadcasted_iota(jnp.int32, (GR, HD), 0)
-    out = jnp.zeros((GR, HD), jnp.float32)
-    for p in range(QPK):
-        q = g * QPK + p
+def head_rows(head_ref, rows, first, count):
+    row = lax.broadcasted_iota(jnp.int32, (rows, HD), 0)
+    out = jnp.zeros((rows, HD), jnp.float32)
+    for p in range(count):
+        q = first + p
         line = head_ref[q * HD : (q + 1) * HD].astype(jnp.float32).reshape(1, HD)
-        out = jnp.where(row == p, jnp.broadcast_to(line, (GR, HD)), out)
+        out = jnp.where(row == p, jnp.broadcast_to(line, (rows, HD)), out)
     return out
+
+
+def heads_of(all_heads, g):
+    row = lax.broadcasted_iota(jnp.int32, all_heads.shape, 0)
+    return jnp.where((row >= g * QPK) & (row < (g + 1) * QPK), all_heads, 0.0).astype(jnp.bfloat16)
 
 
 def pack_tail(parts, r):
@@ -66,15 +72,22 @@
     return tail
 
 
+def rows_of(q, rows):
+    row = lax.broadcasted_iota(jnp.int32, (BOTH, rows), 0)
+    return (row == q) | (row == QR + (q // QPK) * GR + q % QPK)
+
+
 def fold_kernel(w_ref, head_ref, out_ref):
     n = out_ref.shape[0]
-    mains, tails = [], []
+    all_heads = head_rows(head_ref, QR, 0, QH)
+    main = jnp.zeros((QR, HD), jnp.float32)
+    tails = []
     for g in range(KVH):
-        head = head_rows(head_ref, g).astype(jnp.bfloat16)
         cols = slice(g * HD, (g + 1) * HD)
-        mains.append(dot(head, w_ref[0:HD, cols], NT))
-        tails.append(dot(head, w_ref[PIECE - HD : PIECE, cols], NT))
-    packed = jnp.concatenate(mains + [pack_tail(tails, 3)], axis=0).astype(jnp.bfloat16)
+        main = main + dot(heads_of(all_heads, g), w_ref[0:HD, cols], NT)
+        own = head_rows(head_ref, GR, g * QPK, QPK).astype(jnp.bfloat16)
+        tails.append(dot(own, w_ref[PIECE - HD : PIECE, cols], NT))
+    packed = jnp.concatenate([main, pack_tail(tails, 3)], axis=0).astype(jnp.bfloat16)
     for i in range(n):
         out_ref[i] = packed
 
@@ -119,7 +132,7 @@
     n = 2 * own_ref.shape[0]
     across, depth = out_ref.shape[:2]
     rows = x_ref.shape[0]
-    group32 = lane_group(HROWS)
+    group24, group32 = lane_group(QR), lane_group(KVH * GR)
     core = lax.axis_index("core")
     place = (lax.axis_index("zh") * AXES["x"] + lax.axis_index("x")) * AXES["core"] + core
 
@@ -128,26 +141,25 @@
         return jnp.where(core == i % 2, own, other)
 
     for k in range(n // 4):
-        main = [piece(4 * k + r, slice(0, HROWS)) for r in range(4)]
-        tail = [piece(4 * k + r, slice(HROWS, PROWS)) for r in range(4)]
+        main = [piece(4 * k + r, slice(0, QR)) for r in range(4)]
+        tail = [piece(4 * k + r, slice(QR, PROWS)) for r in range(4)]
         for q in range(5):
-            tile = turn(main[q], TAIL * q) if q < 4 else None
+            tile = jnp.zeros((QR, HD), jnp.float32)
+            tails = jnp.zeros((KVH * GR, HD), jnp.float32)
+            if q < 4:
+                tile = jnp.where(group24 >= q, turn(main[q], TAIL * q), tile)
             if q >= 1:
                 r = q - 1
-                tails = jnp.concatenate([turn(tail[r], TAIL * (r - g)) for g in range(KVH)], axis=0)
-                tile = tails if tile is None else jnp.where(group32 >= q, tile, tails)
-                if r >= 1:
-                    tile = jnp.where(group32 < r, turn(main[r], TAIL * r), tile)
+                tile = jnp.where(group24 < r, turn(main[r], TAIL * r), tile)
+                moved = jnp.concatenate([turn(tail[r], TAIL * (r - g)) for g in range(KVH)], axis=0)
+                tails = jnp.where(group32 == r, moved, tails)
             j = 5 * k + q
-            wht_ref[:, j * HD : (j + 1) * HD] = tile.astype(jnp.bfloat16)
-    u = dot(wht_ref[...], x_ref[...], NT)
-    u2 = jnp.concatenate(split(u), axis=0)
-    row64 = lax.broadcasted_iota(jnp.int32, (2 * HROWS, rows), 0) % HROWS
-    zero64 = jnp.zeros((2 * HROWS, rows), jnp.bfloat16)
-    acc = jnp.zeros((2 * HROWS, rows), jnp.float32)
+            wht_ref[:, j * HD : (j + 1) * HD] = jnp.concatenate([tile, tails], axis=0).astype(jnp.bfloat16)
+    u = dot(wht_ref[...], x_ref[...], NT).astype(jnp.bfloat16)
+    zero = jnp.zeros((BOTH, rows), jnp.bfloat16)
+    acc = jnp.zeros((BOTH, rows), jnp.float32)
     for q in range(QH):
-        own = (q // QPK) * GR + q % QPK
-        acc = acc + dot(jnp.where(row64 == own, u2, zero64), p_ref[q], NN)
+        acc = acc + dot(jnp.where(rows_of(q, rows), u, zero), p_ref[q], NN)
     values = jnp.sum(acc, axis=0, keepdims=True)
     val_ref[...] = values
     row8 = lax.broadcasted_iota(jnp.int32, (GR, HD), 0)
@@ -162,24 +174,19 @@
         term = jnp.where(row8 == QPK, high, jnp.where(row8 == QPK + 1, middle, low))
         means = jnp.where((lane8 == SEQ_DEV * place + j) & (row8 >= QPK), term, means)
     resid = jnp.where(mask_ref[...] == 1, values - target_ref[...], 0.0) * grad_scale
-    r_high, r_low = split(resid)
-    both = jnp.concatenate(
-        [jnp.broadcast_to(r_high, (HROWS, rows)), jnp.broadcast_to(r_low, (HROWS, rows))], axis=0
-    )
-    acc = jnp.zeros((2 * HROWS, rows), jnp.float32)
+    every = jnp.broadcast_to(resid, (BOTH, rows)).astype(jnp.bfloat16)
+    acc = jnp.zeros((BOTH, rows), jnp.float32)
     for q in range(QH):
-        own = (q // QPK) * GR + q % QPK
-        acc = acc + dot(jnp.where(row64 == own, both, zero64), p_ref[q], NT)
-    c2 = jnp.concatenate(split(acc[0:HROWS] + acc[HROWS:]), axis=0)
-    g2 = dot(c2, x_ref[...], NN)
-    gt_ref[...] = g2[0:HROWS] + g2[HROWS:]
+        acc = acc + dot(jnp.where(rows_of(q, rows), every, zero), p_ref[q], NT)
+    gt_ref[...] = dot(acc.astype(jnp.bfloat16), x_ref[...], NN)
     for k in range(n // 4):
-        tiles = [gt_ref[:, (5 * k + q) * HD : (5 * k + q + 1) * HD] for q in range(5)]
+        tiles = [gt_ref[0:QR, (5 * k + q) * HD : (5 * k + q + 1) * HD] for q in range(5)]
         for r in range(4):
             main = tiles[r]
             if r:
-                main = jnp.where(group32 < 4 - r, turn(tiles[r], -TAIL * r), turn(tiles[r + 1], -TAIL * r))
-            tail = pack_tail([tiles[r + 1][g * GR : (g + 1) * GR] for g in range(KVH)], r) + means
+                main = jnp.where(group24 < 4 - r, turn(tiles[r], -TAIL * r), turn(tiles[r + 1], -TAIL * r))
+            cols = slice((5 * k + r + 1) * HD, (5 * k + r + 2) * HD)
+            tail = pack_tail([gt_ref[QR + g * GR : QR + (g + 1) * GR, cols] for g in range(KVH)], r) + means
             i = 4 * k + r
             out_ref[i % across, i // across] = jnp.concatenate([main, tail], axis=0).astype(jnp.bfloat16)
 
@@ -202,12 +209,12 @@
         out_ref[i] = total
 
 
-def seq_kernel(plan_ref, in_ref, own_ref, seq_ref, val_ref):
+def last_kernel(plan_ref, line_ref, own_ref, head_ref, in_ref, seq_ref, val_ref, out_ref):
     val_ref[...] = own_ref[...]
     mine = lax.axis_index("zl")
     block = jnp.zeros((GR, HD), jnp.float32)
     for h in range(AXES["zh"]):
-        block = block + in_ref[h * AXES["zl"] + mine, HROWS:PROWS, :].astype(jnp.float32)
+        block = block + line_ref[h * AXES["zl"] + mine, QR:PROWS, :].astype(jnp.float32)
     row8 = lax.broadcasted_iota(jnp.int32, (GR, HD), 0)
     mean = jnp.sum(jnp.where(row8 >= QPK, block, 0.0), axis=0, keepdims=True)
     slot = lax.broadcasted_iota(jnp.int32, (1, HD), 1)
@@ -218,20 +225,18 @@
         out = jnp.where(lane == i, own, out)
     seq_ref[...] = out
 
-
-def weight_kernel(head_ref, in_ref, out_ref):
     total = jnp.sum(in_ref[...].astype(jnp.float32), axis=0)
-    main = total[0:HROWS]
-    tail = jnp.concatenate([turn(total[HROWS:PROWS], -TAIL * g) for g in range(KVH)], axis=0)
-    main2 = jnp.concatenate(split(main), axis=0)
-    tail2 = jnp.concatenate(split(tail), axis=0)
+    main2 = two_terms(total[0:QR])
+    all_heads = head_rows(head_ref, QR, 0, QH)
     for g in range(KVH):
-        head = head_rows(head_ref, g).astype(jnp.bfloat16)
-        blank = jnp.zeros((GR, HD), jnp.bfloat16)
-        block = jnp.concatenate([head if i == g else blank for i in range(KVH)] * 2, axis=0)
         cols = slice(g * HD, (g + 1) * HD)
-        out_ref[0:HD, cols] = dot(main2, block, TN).astype(jnp.bfloat16)
-        out_ref[HD:PIECE, cols] = dot(tail2, block, TN)[0:TAIL].astype(jnp.bfloat16)
+        wide = heads_of(all_heads, g).astype(jnp.float32)
+        wide2 = jnp.concatenate([wide, wide], axis=0).astype(jnp.bfloat16)
+        out_ref[0:HD, cols] = dot(main2, wide2, TN).astype(jnp.bfloat16)
+        small = head_rows(head_ref, GR, g * QPK, QPK)
+        small2 = jnp.concatenate([small, small], axis=0).astype(jnp.bfloat16)
+        tail2 = two_terms(turn(total[QR:PROWS], -TAIL * g))
+        out_ref[HD:PIECE, cols] = dot(tail2, small2, TN)[0:TAIL].astype(jnp.bfloat16)
 
 
 def local(hidden, queries, keys, value_weight, value_head, lengths, plan, targets, loss_mask):
@@ -291,7 +296,7 @@
             jax.ShapeDtypeStruct((1, rows), f32),
             jax.ShapeDtypeStruct((n // AXES["zh"], AXES["zh"], PROWS, HD), bf16),
         ],
-        scratch_shapes=[pltpu.VMEM((HROWS, d), bf16), pltpu.VMEM((HROWS, d), f32)],
+        scratch_shapes=[pltpu.VMEM((BOTH, d), bf16), pltpu.VMEM((BOTH, d), f32)],
         compiler_params=VMEM,
         name="main",
     )(seen, share, own_core, other_core, hidden[0], probs, targets, loss_mask)
@@ -313,21 +318,17 @@
     )(lines)
     sums = lax.all_to_all(copies, "y", 0, 0)
 
-    seq_values, values = pl.pallas_call(
-        seq_kernel,
-        in_specs=[smem, vmem, vmem],
-        out_shape=[jax.ShapeDtypeStruct((1, SEQ_DEV), f32), jax.ShapeDtypeStruct((1, rows), f32)],
-        compiler_params=VMEM,
-        cost_estimate=pl.CostEstimate(flops=2**20, bytes_accessed=2**20, transcendentals=0),
-        name="seq",
-    )(plan, lines, own_values)
-
-    d_weight = pl.pallas_call(
-        weight_kernel,
-        out_shape=jax.ShapeDtypeStruct(value_weight.shape, bf16),
-        compiler_params=VMEM,
-        name="weight",
-    )(value_head, sums)
+    seq_values, values, d_weight = pl.pallas_call(
+        last_kernel,
+        in_specs=[smem] + [vmem] * 4,
+        out_shape=[
+            jax.ShapeDtypeStruct((1, SEQ_DEV), f32),
+            jax.ShapeDtypeStruct((1, rows), f32),
+            jax.ShapeDtypeStruct(value_weight.shape, bf16),
+        ],
+        compiler_params=VMEM,
+        name="last",
+    )(plan, lines, own_values, value_head, sums)
     return values, seq_values, d_weight
 
 

time: 85.4 us -> 83.1 us (0.973)
  blocking collectives: 26.2 us -> 40.9 us
  waiting for transfers between devices: 16.5 us -> 7.98 us
  starting transfers between devices: 26.8 us -> 19.7 us
  Pallas kernels: 14.6 us -> 13.4 us
    all_to_all x0 -> x1, blocking collectives: none -> 15.3 us  [local(): sums = lax.all_to_all(copies, 'y', 0, 0)]
    all_to_all x1 -> x0, waiting for transfers between devices: 7.39 us -> none  [local(): sums = lax.all_to_all(copies, 'y', 0, 0)]
    all_to_all x1 -> x0, starting transfers between devices: 7.1 us -> none  [local(): sums = lax.all_to_all(copies, 'y', 0, 0)]
    all_to_all x1, waiting for transfers between devices: 7.8 us -> 6.69 us  [local(): own_core = lax.all_to_all(folded, ('zh', 'x'), 0, 0)]
    pallas_call x2 -> x1, Pallas kernels: 2.13 us -> 1.5 us  [local(): pl.pallas_call(last_kernel, in_specs=[smem] + [vmem] * 4, out_shape=[jax....]
  transfers between devices with their start and end apart: 3 -> 2, of which waited for: 3 -> 2; matrix products, arithmetic and copies ran while one was open for 0% -> 0% of each run, Pallas kernels for 7% -> 6%
where the time goes in v4:
time: 83.1 us; the launch traced here: 82.7 us
  blocking collectives  40.9 us (49%)
  starting transfers between devices  19.7 us (24%)
  Pallas kernels  13.4 us (16%)
  waiting for transfers between devices  7.98 us (10%)
    all_to_all x1, starting transfers between devices, local(): own_core = lax.all_to_all(folded, ('zh', 'x'), 0, 0)  17.5 us
    all_to_all x1, blocking collectives, local(): sums = lax.all_to_all(copies, 'y', 0, 0)  15.3 us
    all_to_all x1, blocking collectives, local(): lines = lax.all_to_all(line, ('zh', 'zl'), 0, 0)  15.2 us
    all_to_all x1, blocking collectives, local(): terms = lax.all_to_all(pieces, ('x', 'core'), 0, 0)  10.4 us
    all_to_all x1, waiting for transfers between devices, local(): own_core = lax.all_to_all(folded, ('zh', 'x'), 0, 0)  6.69 us
    pallas_call x1, Pallas kernels, local(): pl.pallas_call(probs_kernel, grid=(KVH,), in_specs=[smem, pl.BlockSpec((r...  5.05 us
    pallas_call x1, Pallas kernels, local(): pl.pallas_call(functools.partial(main_kernel, grad_scale), in_specs=[pl.B...  4.72 us
    ppermute x1, starting transfers between devices, local(): other_core = lax.ppermute(own_core, 'core', [(0, 1), (1, 0)])  2.17 us
  transfers between devices with their start and end apart: 2, of which 2 were waited for; matrix products, arithmetic and copies ran while one was open for 0% of the time, Pallas kernels for 6%

profile of v4, /device:TPU:2, one launch (start us, length us, event | category | flops | bytes accessed | tf_op | source)
XLA Modules:
  0.0 82.7 jit_solution(16934889304849703760)
XLA Ops:
  0.6 0.0 copy-start
  0.6 2.0 %fold.1 = bf16[16,32,128]{2,1,0:T(8,128)(2,1)} custom-call(bf16[160,512]{1,0:T(8,128)(2,1)} %w_ref.1, bf16[2560]{0:T(1024)(128)(2,1)} %head_ref.3), custom_call_target="tpu_custom_call" | custom-call | tf_op jit(solution)/shard_map/fold/pallas_call | solution.py:252
  2.7 17.5 %all-to-all-start = ((bf16[16,32,128]{2,1,0:T(8,128)(2,1)}), bf16[16,32,128]{2,1,0:T(8,128)(2,1)S(1)}, u32[]{:S(2)}, u32[]{:S(2)}) async-start(bf16[16,32,128]{2,1,0:T(8,128)(2,1)} %fold.1), calls=%async_computation | async-start | bytes 262144 | tf_op jit(solution)/shard_map/all_to_all | solution.py:258
  20.2 0.0 copy-start.4
  20.2 0.0 copy-start.5
  20.2 5.1 %probs.1 = (bf16[20,256,256]{2,1,0:T(8,128)(2,1)}, f32[8,256]{1,0:T(8,128)}) custom-call(s32[1,4]{1,0:T(1,128)} %bitcast.8, bf16[256,2560]{1,0:T(8,128)(2,1)} %bitcast.6, bf16[256,512]{1,0:T(8,128)(2,1)} %bitcast.7), custom_call_target="tpu_custom_call" | custom-call | flops 335544320 | bytes 6291456 | tf_op jit(solution)/shard_map/probs/pallas_call | solution.py:259
  25.2 0.0 copy-start.3
  25.2 6.7 %all-to-all-done.own_ref = bf16[16,32,128]{2,1,0:T(8,128)(2,1)S(1)} async-done(((bf16[16,32,128]{2,1,0:T(8,128)(2,1)}), bf16[16,32,128]{2,1,0:T(8,128)(2,1)S(1)}, u32[]{:S(2)}, u32[]{:S(2)}) %all-to-all-start) | async-done | bytes 131104 | tf_op jit(solution)/shard_map/all_to_all | solution.py:258
  31.9 2.2 %collective-permute-start = (bf16[16,32,128]{2,1,0:T(8,128)(2,1)S(1)}, bf16[16,32,128]{2,1,0:T(8,128)(2,1)S(1)}, u32[]{:S(2)}, u32[]{:S(2)}) collective-permute-start(bf16[16,32,128]{2,1,0:T(8,128)(2,1)S(1)} %all-to-all-done.own_ref), channel_id=1, source_target_pairs={{0,24},{24,0},{1,25},{25,1},{2,26},{26,2},{3,27},{27,3},{4,28},{28... | collective-permute-start | bytes 393224 | tf_op jit(solution)/shard_map/ppermute | solution.py:281
  34.1 0.0 copy-done
  34.1 1.3 %collective-permute-done.other_ref = bf16[16,32,128]{2,1,0:T(8,128)(2,1)S(1)} collective-permute-done((bf16[16,32,128]{2,1,0:T(8,128)(2,1)S(1)}, bf16[16,32,128]{2,1,0:T(8,128)(2,1)S(1)}, u32[]{:S(2)}, u32[]{:S(2)}) %collective-permute-start) | collective-permute-done | bytes 131104 | tf_op jit(solution)/shard_map/ppermute | solution.py:281
  35.4 0.0 copy-done.4
  35.4 0.0 copy-done.5
  35.4 0.0 copy-done.3
  35.4 0.0 copy-done.1
  35.4 0.0 copy-start.2
  35.5 0.0 copy-start.6
  35.5 4.7 %main.1 = (f32[1,256]{1,0:T(1,128)S(1)}, bf16[8,4,32,128]{3,2,1,0:T(8,128)(2,1)S(1)}) custom-call(f32[8,128]{1,0:T(8,128)S(1)} %seen.1.seen_ref, f32[8,256]{1,0:T(8,128)S(1)} %copy-done.3, bf16[16,32,128]{2,1,0:T(8,128)(2,1)S(1)} %all-to-all-done.own_ref, bf16[16,32,128]{2,1,0:T(8,128)(2,1)S(1)} %collective-permute-done.other_ref, ...), custom_call_target="tpu_custom_call" | custom-call | tf_op jit(solution)/shard_map/main/pallas_call | solution.py:292
  40.2 10.4 %all_to_all.20.in_ref = bf16[8,4,32,128]{3,2,1,0:T(8,128)(2,1)S(1)} all-to-all(bf16[8,4,32,128]{3,2,1,0:T(8,128)(2,1)S(1)} %get-tuple-element.16), channel_id=1, replica_groups=mesh['zh'=4,'x'=4,'core'=2,'y'=8,'zl'=3] {'x','core'}, dimensions={0} | all-to-all | bytes 524288 | tf_op jit(solution)/shard_map/all_to_all | solution.py:303
  50.7 15.2 %all_to_all.21.in_ref.line_ref = bf16[12,32,128]{2,1,0:T(8,128)(2,1)S(1)} all-to-all(bf16[12,32,128]{2,1,0:T(8,128)(2,1)S(1)} %line.1), channel_id=1, replica_groups=mesh['zh'=4,'x'=4,'core'=2,'y'=8,'zl'=3] {'zh','zl'}, dimensions={0} | all-to-all | bytes 196608 | tf_op jit(solution)/shard_map/all_to_all | solution.py:311
  65.9 15.3 %all_to_all.22.in_ref = bf16[8,32,128]{2,1,0:T(8,128)(2,1)S(1)} all-to-all(bf16[8,32,128]{2,1,0:T(8,128)(2,1)S(1)} %group.1), channel_id=1, replica_groups=mesh['zh'=4,'x'=4,'core'=2,'y'=8,'zl'=3] {'y'}, dimensions={0} | all-to-all | bytes 131072 | tf_op jit(solution)/shard_map/all_to_all | solution.py:319
  81.2 0.0 copy-done.2
  81.2 0.0 copy-done.6
  81.2 1.5 %last.1 = (f32[1,4]{1,0:T(1,128)}, f32[1,256]{1,0:T(1,128)}, bf16[160,512]{1,0:T(8,128)(2,1)}) custom-call(s32[1,4]{1,0:T(1,128)S(1)} %copy-done.6, bf16[12,32,128]{2,1,0:T(8,128)(2,1)S(1)} %all_to_all.21.in_ref.line_ref, f32[1,256]{1,0:T(1,128)S(1)} %get-tuple-element.17.own_ref, bf16[2560]{0:T(1024)(128)(2,1)S(1)} %copy-done.2, ...), custom_call_target="tpu_custom_call" | custom-call | tf_op jit(solution)/shard_map/last/pallas_call | solution.py:321
  (4 shorter events, 0.1 us)
Async XLA Ops:
  0.6 33.5 %copy-start = (bf16[1,256,5120]{2,1,0:T(8,128)(2,1)S(1)}, bf16[1,256,5120]{2,1,0:T(8,128)(2,1)}, u32[]{:S(2)}) copy-start(bf16[1,256,5120]{2,1,0:T(8,128)(2,1)} %param.9) | copy-start | bytes 7864324
  2.7 29.3 %all-to-all-start = ((bf16[16,32,128]{2,1,0:T(8,128)(2,1)}), bf16[16,32,128]{2,1,0:T(8,128)(2,1)S(1)}, u32[]{:S(2)}, u32[]{:S(2)}) async-start(bf16[16,32,128]{2,1,0:T(8,128)(2,1)} %fold.1), calls=%async_computation | async-start | bytes 262144 | tf_op jit(solution)/shard_map/all_to_all | solution.py:258
  20.2 15.3 %copy-start.4 = (f32[1,256]{1,0:T(1,128)S(1)}, f32[1,256]{1,0:T(1,128)}, u32[]{:S(2)}) copy-start(f32[1,256]{1,0:T(1,128)} %target_ref.1) | copy-start | bytes 3076
  20.2 15.3 %copy-start.5 = (s32[1,256]{1,0:T(1,128)S(1)}, s32[1,256]{1,0:T(1,128)}, u32[]{:S(2)}) copy-start(s32[1,256]{1,0:T(1,128)} %mask_ref.1) | copy-start | bytes 3076
  25.2 10.2 %copy-start.3 = (f32[8,256]{1,0:T(8,128)S(1)}, f32[8,256]{1,0:T(8,128)}, u32[]{:S(2)}) copy-start(f32[8,256]{1,0:T(8,128)} %get-tuple-element.14.share_ref) | copy-start | bytes 24580
  31.9 3.5 %copy-start.1 = (bf16[20,256,256]{2,1,0:T(8,128)(2,1)S(1)}, bf16[20,256,256]{2,1,0:T(8,128)(2,1)}, u32[]{:S(2)}) copy-start(bf16[20,256,256]{2,1,0:T(8,128)(2,1)} %get-tuple-element.15.p_ref) | copy-start | bytes 7864324
  31.9 3.5 %collective-permute-start = (bf16[16,32,128]{2,1,0:T(8,128)(2,1)S(1)}, bf16[16,32,128]{2,1,0:T(8,128)(2,1)S(1)}, u32[]{:S(2)}, u32[]{:S(2)}) collective-permute-start(bf16[16,32,128]{2,1,0:T(8,128)(2,1)S(1)} %all-to-all-done.own_ref), channel_id=1, source_target_pairs={{0,24},{24,0},{1,25},{25,1},{2,26},{26,2},{3,27},{27,3},{4,28},{28... | collective-permute-start | bytes 393224 | tf_op jit(solution)/shard_map/ppermute | solution.py:281
  35.4 45.7 %copy-start.2 = (bf16[2560]{0:T(1024)(128)(2,1)S(1)}, bf16[2560]{0:T(1024)(128)(2,1)}, u32[]{:S(2)}) copy-start(bf16[2560]{0:T(1024)(128)(2,1)} %head_ref.3) | copy-start | bytes 15364
  35.5 45.7 %copy-start.6 = (s32[1,4]{1,0:T(1,128)S(1)}, s32[1,4]{1,0:T(1,128)}, u32[]{:S(2)}) copy-start(s32[1,4]{1,0:T(1,128)} %plan_ref.1) | copy-start | bytes 52

commit v5 on v4

--- a/solution.py
+++ b/solution.py
@@ -116,14 +116,16 @@
             begin = begin + size
         share_ref[...] = share
 
-    bias = bias_ref[...]
     scale = math.log2(math.e) / math.sqrt(HD)
+    half = rows // 2
     for p in range(QPK):
-        score = dot(k_ref[...], q_ref[:, p * HD : (p + 1) * HD], NT) + bias
-        top = jnp.max(score, axis=0, keepdims=True)
-        expo = jnp.exp2((score - top) * scale)
-        total = jnp.sum(expo, axis=0, keepdims=True)
-        out_ref[p] = (expo * (1.0 / total)).astype(jnp.bfloat16)
+        for t, s in ((slice(0, half), slice(0, half)), (slice(half, rows), slice(0, rows))):
+            score = dot(k_ref[s, :], q_ref[t, p * HD : (p + 1) * HD], NT) + bias_ref[s, t]
+            top = jnp.max(score, axis=0, keepdims=True)
+            expo = jnp.exp2((score - top) * scale)
+            total = jnp.sum(expo, axis=0, keepdims=True)
+            out_ref[p, s, t] = (expo * (1.0 / total)).astype(jnp.bfloat16)
+        out_ref[p, half:rows, 0:half] = jnp.zeros((half, half), jnp.bfloat16)
 
 
 def main_kernel(
@@ -221,7 +223,7 @@
     lane = lax.broadcasted_iota(jnp.int32, (1, SEQ_DEV), 1)
     out = jnp.zeros((1, SEQ_DEV), jnp.float32)
     for i in range(SEQ_DEV):
-        own = jnp.sum(jnp.where(slot == plan_ref[0, i], mean, 0.0), axis=1, keepdims=True)
+        own = jnp.sum(jnp.where(slot == plan_ref[0:1, i : i + 1], mean, 0.0), axis=1, keepdims=True)
         out = jnp.where(lane == i, own, out)
     seq_ref[...] = out
 
@@ -320,7 +322,7 @@
 
     seq_values, values, d_weight = pl.pallas_call(
         last_kernel,
-        in_specs=[smem] + [vmem] * 4,
+        in_specs=[vmem] * 5,
         out_shape=[
             jax.ShapeDtypeStruct((1, SEQ_DEV), f32),
             jax.ShapeDtypeStruct((1, rows), f32),

time: 83.1 us -> 82.6 us (level)
  no operation moved by 1% of the time
where the time goes in v5:
time: 82.6 us; the launch traced here: 82.2 us
  blocking collectives  40.9 us (50%)
  starting transfers between devices  19.7 us (24%)
  Pallas kernels  12.6 us (15%)
  waiting for transfers between devices  8.2 us (10%)
    all_to_all x1, starting transfers between devices, local(): own_core = lax.all_to_all(folded, ('zh', 'x'), 0, 0)  17.5 us
    all_to_all x1, blocking collectives, local(): sums = lax.all_to_all(copies, 'y', 0, 0)  15.3 us
    all_to_all x1, blocking collectives, local(): lines = lax.all_to_all(line, ('zh', 'zl'), 0, 0)  15.2 us
    all_to_all x1, blocking collectives, local(): terms = lax.all_to_all(pieces, ('x', 'core'), 0, 0)  10.4 us
    all_to_all x1, waiting for transfers between devices, local(): own_core = lax.all_to_all(folded, ('zh', 'x'), 0, 0)  6.91 us
    pallas_call x1, Pallas kernels, local(): pl.pallas_call(probs_kernel, grid=(KVH,), in_specs=[smem, pl.BlockSpec((r...  4.84 us
    pallas_call x1, Pallas kernels, local(): pl.pallas_call(functools.partial(main_kernel, grad_scale), in_specs=[pl.B...  4.72 us
    ppermute x1, starting transfers between devices, local(): other_core = lax.ppermute(own_core, 'core', [(0, 1), (1, 0)])  2.17 us
  transfers between devices with their start and end apart: 2, of which 2 were waited for; matrix products, arithmetic and copies ran while one was open for 0% of the time, Pallas kernels for 6%

profile of v5, /device:TPU:2, one launch (start us, length us, event | category | flops | bytes accessed | tf_op | source)
XLA Modules:
  0.0 82.2 jit_solution(3987810696958159472)
XLA Ops:
  0.6 0.0 copy-start
  0.6 2.0 %fold.1 = bf16[16,32,128]{2,1,0:T(8,128)(2,1)} custom-call(bf16[160,512]{1,0:T(8,128)(2,1)} %w_ref.1, bf16[2560]{0:T(1024)(128)(2,1)} %head_ref.3), custom_call_target="tpu_custom_call" | custom-call | tf_op jit(solution)/shard_map/fold/pallas_call | solution.py:254
  2.7 17.5 %all-to-all-start = ((bf16[16,32,128]{2,1,0:T(8,128)(2,1)}), bf16[16,32,128]{2,1,0:T(8,128)(2,1)S(1)}, u32[]{:S(2)}, u32[]{:S(2)}) async-start(bf16[16,32,128]{2,1,0:T(8,128)(2,1)} %fold.1), calls=%async_computation | async-start | bytes 262144 | tf_op jit(solution)/shard_map/all_to_all | solution.py:260
  20.2 0.0 copy-start.4
  20.2 0.0 copy-start.5
  20.2 4.8 %probs.1 = (bf16[20,256,256]{2,1,0:T(8,128)(2,1)}, f32[8,256]{1,0:T(8,128)}) custom-call(s32[1,4]{1,0:T(1,128)} %bitcast.8, bf16[256,2560]{1,0:T(8,128)(2,1)} %bitcast.6, bf16[256,512]{1,0:T(8,128)(2,1)} %bitcast.7), custom_call_target="tpu_custom_call" | custom-call | flops 335544320 | bytes 6291456 | tf_op jit(solution)/shard_map/probs/pallas_call | solution.py:261
  25.0 0.0 copy-start.3
  25.0 6.9 %all-to-all-done.own_ref = bf16[16,32,128]{2,1,0:T(8,128)(2,1)S(1)} async-done(((bf16[16,32,128]{2,1,0:T(8,128)(2,1)}), bf16[16,32,128]{2,1,0:T(8,128)(2,1)S(1)}, u32[]{:S(2)}, u32[]{:S(2)}) %all-to-all-start) | async-done | bytes 131104 | tf_op jit(solution)/shard_map/all_to_all | solution.py:260
  31.9 2.2 %collective-permute-start = (bf16[16,32,128]{2,1,0:T(8,128)(2,1)S(1)}, bf16[16,32,128]{2,1,0:T(8,128)(2,1)S(1)}, u32[]{:S(2)}, u32[]{:S(2)}) collective-permute-start(bf16[16,32,128]{2,1,0:T(8,128)(2,1)S(1)} %all-to-all-done.own_ref), channel_id=1, source_target_pairs={{0,24},{24,0},{1,25},{25,1},{2,26},{26,2},{3,27},{27,3},{4,28},{28... | collective-permute-start | bytes 393224 | tf_op jit(solution)/shard_map/ppermute | solution.py:283
  34.1 0.0 copy-done
  34.1 1.3 %collective-permute-done.other_ref = bf16[16,32,128]{2,1,0:T(8,128)(2,1)S(1)} collective-permute-done((bf16[16,32,128]{2,1,0:T(8,128)(2,1)S(1)}, bf16[16,32,128]{2,1,0:T(8,128)(2,1)S(1)}, u32[]{:S(2)}, u32[]{:S(2)}) %collective-permute-start) | collective-permute-done | bytes 131104 | tf_op jit(solution)/shard_map/ppermute | solution.py:283
  35.4 0.0 copy-done.4
  35.4 0.0 copy-done.5
  35.4 0.0 copy-done.3
  35.4 0.0 copy-done.1
  35.4 0.0 copy-start.2
  35.5 0.0 copy-start.6
  35.5 4.7 %main.1 = (f32[1,256]{1,0:T(1,128)S(1)}, bf16[8,4,32,128]{3,2,1,0:T(8,128)(2,1)S(1)}) custom-call(f32[8,128]{1,0:T(8,128)S(1)} %seen.1.seen_ref, f32[8,256]{1,0:T(8,128)S(1)} %copy-done.3, bf16[16,32,128]{2,1,0:T(8,128)(2,1)S(1)} %all-to-all-done.own_ref, bf16[16,32,128]{2,1,0:T(8,128)(2,1)S(1)} %collective-permute-done.other_ref, ...), custom_call_target="tpu_custom_call" | custom-call | tf_op jit(solution)/shard_map/main/pallas_call | solution.py:294
  40.2 10.4 %all_to_all.20.in_ref = bf16[8,4,32,128]{3,2,1,0:T(8,128)(2,1)S(1)} all-to-all(bf16[8,4,32,128]{3,2,1,0:T(8,128)(2,1)S(1)} %get-tuple-element.16), channel_id=1, replica_groups=mesh['zh'=4,'x'=4,'core'=2,'y'=8,'zl'=3] {'x','core'}, dimensions={0} | all-to-all | bytes 524288 | tf_op jit(solution)/shard_map/all_to_all | solution.py:305
  50.7 15.2 %all_to_all.21.in_ref.line_ref = bf16[12,32,128]{2,1,0:T(8,128)(2,1)S(1)} all-to-all(bf16[12,32,128]{2,1,0:T(8,128)(2,1)S(1)} %line.1), channel_id=1, replica_groups=mesh['zh'=4,'x'=4,'core'=2,'y'=8,'zl'=3] {'zh','zl'}, dimensions={0} | all-to-all | bytes 196608 | tf_op jit(solution)/shard_map/all_to_all | solution.py:313
  65.9 15.3 %all_to_all.22.in_ref = bf16[8,32,128]{2,1,0:T(8,128)(2,1)S(1)} all-to-all(bf16[8,32,128]{2,1,0:T(8,128)(2,1)S(1)} %group.1), channel_id=1, replica_groups=mesh['zh'=4,'x'=4,'core'=2,'y'=8,'zl'=3] {'y'}, dimensions={0} | all-to-all | bytes 131072 | tf_op jit(solution)/shard_map/all_to_all | solution.py:321
  81.2 0.0 copy-done.2
  81.2 0.0 copy-done.6
  81.2 1.0 %last.1 = (f32[1,4]{1,0:T(1,128)}, f32[1,256]{1,0:T(1,128)}, bf16[160,512]{1,0:T(8,128)(2,1)}) custom-call(s32[1,4]{1,0:T(1,128)S(1)} %copy-done.6, bf16[12,32,128]{2,1,0:T(8,128)(2,1)S(1)} %all_to_all.21.in_ref.line_ref, f32[1,256]{1,0:T(1,128)S(1)} %get-tuple-element.17.own_ref, bf16[2560]{0:T(1024)(128)(2,1)S(1)} %copy-done.2, ...), custom_call_target="tpu_custom_call" | custom-call | tf_op jit(solution)/shard_map/last/pallas_call | solution.py:323
  (4 shorter events, 0.1 us)
Async XLA Ops:
  0.6 33.5 %copy-start = (bf16[1,256,5120]{2,1,0:T(8,128)(2,1)S(1)}, bf16[1,256,5120]{2,1,0:T(8,128)(2,1)}, u32[]{:S(2)}) copy-start(bf16[1,256,5120]{2,1,0:T(8,128)(2,1)} %param.9) | copy-start | bytes 7864324
  2.7 29.3 %all-to-all-start = ((bf16[16,32,128]{2,1,0:T(8,128)(2,1)}), bf16[16,32,128]{2,1,0:T(8,128)(2,1)S(1)}, u32[]{:S(2)}, u32[]{:S(2)}) async-start(bf16[16,32,128]{2,1,0:T(8,128)(2,1)} %fold.1), calls=%async_computation | async-start | bytes 262144 | tf_op jit(solution)/shard_map/all_to_all | solution.py:260
  20.2 15.3 %copy-start.4 = (f32[1,256]{1,0:T(1,128)S(1)}, f32[1,256]{1,0:T(1,128)}, u32[]{:S(2)}) copy-start(f32[1,256]{1,0:T(1,128)} %target_ref.1) | copy-start | bytes 3076
  20.2 15.3 %copy-start.5 = (s32[1,256]{1,0:T(1,128)S(1)}, s32[1,256]{1,0:T(1,128)}, u32[]{:S(2)}) copy-start(s32[1,256]{1,0:T(1,128)} %mask_ref.1) | copy-start | bytes 3076
  25.0 10.4 %copy-start.3 = (f32[8,256]{1,0:T(8,128)S(1)}, f32[8,256]{1,0:T(8,128)}, u32[]{:S(2)}) copy-start(f32[8,256]{1,0:T(8,128)} %get-tuple-element.14.share_ref) | copy-start | bytes 24580
  31.9 3.5 %copy-start.1 = (bf16[20,256,256]{2,1,0:T(8,128)(2,1)S(1)}, bf16[20,256,256]{2,1,0:T(8,128)(2,1)}, u32[]{:S(2)}) copy-start(bf16[20,256,256]{2,1,0:T(8,128)(2,1)} %get-tuple-element.15.p_ref) | copy-start | bytes 7864324
  31.9 3.5 %collective-permute-start = (bf16[16,32,128]{2,1,0:T(8,128)(2,1)S(1)}, bf16[16,32,128]{2,1,0:T(8,128)(2,1)S(1)}, u32[]{:S(2)}, u32[]{:S(2)}) collective-permute-start(bf16[16,32,128]{2,1,0:T(8,128)(2,1)S(1)} %all-to-all-done.own_ref), channel_id=1, source_target_pairs={{0,24},{24,0},{1,25},{25,1},{2,26},{26,2},{3,27},{27,3},{4,28},{28... | collective-permute-start | bytes 393224 | tf_op jit(solution)/shard_map/ppermute | solution.py:283
  35.4 45.7 %copy-start.2 = (bf16[2560]{0:T(1024)(128)(2,1)S(1)}, bf16[2560]{0:T(1024)(128)(2,1)}, u32[]{:S(2)}) copy-start(bf16[2560]{0:T(1024)(128)(2,1)} %head_ref.3) | copy-start | bytes 15364
  35.5 45.7 %copy-start.6 = (s32[1,4]{1,0:T(1,128)S(1)}, s32[1,4]{1,0:T(1,128)}, u32[]{:S(2)}) copy-start(s32[1,4]{1,0:T(1,128)} %plan_ref.1) | copy-start | bytes 52
